TPU v7x, 256 devices: a whole 4x4x8 slice. The times are simulated.
256 devices in a mesh: facet: 32 (over x, z_lo, y), col: 8 (over z_hi, core).
Axes of the slice: x: 4, y: 4, z: 8 (z_hi: 4, z_lo: 2; z = z_hi * 2 + z_lo), core: 2. Of those that a mesh axis runs over, the one named last changes fastest.
Arguments:
- facet_strips: bfloat16 [16384, 2, 1024], P('facet', None, 'col'), may hold values from -6 to 6
- facet_off: int32 [4], replicated, may hold values from 0 to 65535
- strip_off: int32 [8], replicated, may hold values from 0 to 65535
- sub_v: int32 [32], replicated, may hold values from 0 to 65535
- sub_u: int32 [8], replicated, may hold values from 0 to 65535
- screen_phase: float32 [2048, 8192], P('facet', 'col'), may hold values from -3.140625 to 3.140625
- visibilities: bfloat16 [512, 8, 2, 8192], P('facet', None, None, 'col'), may hold values from -6 to 6
- block_band: int32 [512, 8], P('facet', 'col'), may hold values from 0 to 7
- vis_weight: float32 [512, 64], P('facet', 'col'), may hold values from 0.2 to 2
Outputs:
- subgrid_residual: bfloat16 [2048, 2, 8192], P('facet', None, 'col')
- facet_residual: bfloat16 [16384, 2, 1024], P('facet', None, 'col')
Inputs may be any that keep to these rules, and one draw needn't show every extreme that they name: `block_band`: each visibility block covers one band of 8 rows of its subgrid's slab.
All inputs are finite; a program needn't handle non-finite values.
Results may differ from a plain program's by a relative error of at most 0.02.
Values may be sent and summed in bfloat16 or wider, within the bound.
A program may use at most 64 MiB of HBM per device.

v0:
```python
import functools
import math

import jax
import jax.numpy as jnp
from jax import lax
from jax.experimental import pallas as pl
from jax.experimental.pallas import tpu as pltpu
from jax.sharding import PartitionSpec as P

MESH = pl.DeviceIdType.MESH
IMG = 65536
TURN = 2.0 * math.pi / IMG
F32 = jnp.float32
BF16 = jnp.bfloat16

K = 32
C = 8
S = 64
Y = 512
X = 128
U = 1024
PIECES = 8
UB = U // X
BLOCKS = 16


def quarter_turns(q, t):
    t2 = t * t
    sin = t + t * t2 * (-1.6666654611e-1 + t2 * (8.3321608736e-3 + t2 * -1.9515295891e-4))
    cos = 1.0 - 0.5 * t2 + t2 * t2 * (
        4.166664568298827e-2 + t2 * (-1.388731625493765e-3 + t2 * 2.443315711809948e-5)
    )
    odd = (q & 1) == 1
    even_cos = jnp.where(odd, sin, cos)
    even_sin = jnp.where(odd, cos, sin)
    return (
        jnp.where(((q + 1) & 2) != 0, -even_cos, even_cos),
        jnp.where((q & 2) != 0, -even_sin, even_sin),
    )


def unit(k):
    k = k & (IMG - 1)
    q = (k + IMG // 8) >> 14
    return quarter_turns(q, (k - (q << 14)).astype(F32) * TURN)


def cos_sin(angle):
    turns = jnp.floor(angle * (2.0 / math.pi) + 0.5)
    t = (angle - turns * 1.5703125) - turns * 4.837512969970703e-4
    t = t - turns * 7.549789948768648e-8
    return quarter_turns(turns.astype(jnp.int32), t)


def iota(shape, dim):
    return lax.broadcasted_iota(jnp.int32, shape, dim)


def facet_step(me, p):
    x = ((me >> 3) + (p >> 3)) & 3
    z = ((me >> 2) ^ (p >> 2)) & 1
    y = (me + p) & 3
    return (x << 3) | (z << 2) | y


def back_step(p):
    x = (0 - (p >> 3)) & 3
    y = (0 - p) & 3
    return (x << 3) | (p & 4) | y


def col_step(me, q):
    z = ((me >> 1) + (q >> 1)) & 3
    return (z << 1) | ((me ^ q) & 1)


def kernel(
    facet_off,
    strip_off,
    sub_v,
    sub_u,
    strips,
    bands,
    screen_hbm,
    vis_hbm,
    residual,
    image,
    g_tab,
    mod,
    wide,
    m_tab,
    part_out,
    part_in,
    own_part,
    asm,
    w_tab,
    d_tab,
    screen,
    vis,
    base,
    weight,
    share_acc,
    share_out,
    share_in,
    share,
    back,
    back_acc,
    load_sem,
    a_send,
    a_recv,
    c_send,
    c_recv,
    e_send,
    e_recv,
    f_send,
    f_recv,
):
    me = lax.axis_index("facet")
    col = lax.axis_index("col")

    screen_load = pltpu.make_async_copy(screen_hbm, screen, load_sem.at[0])
    vis_load = pltpu.make_async_copy(vis_hbm, vis, load_sem.at[1])
    screen_load.start()
    vis_load.start()

    barrier = pltpu.get_barrier_semaphore()

    def greet_facet(p, carry):
        pl.semaphore_signal(
            barrier, inc=1, device_id=(facet_step(me, p), col), device_id_type=MESH
        )
        return carry

    def greet_col(q, carry):
        pl.semaphore_signal(
            barrier, inc=1, device_id=(me, col_step(col, q)), device_id_type=MESH
        )
        return carry

    lax.fori_loop(1, K, greet_facet, 0)
    lax.fori_loop(1, C, greet_col, 0)

    off = facet_off[me // PIECES]
    first = off + (me % PIECES) * Y

    def g_rows(i, carry):
        row = iota((8, Y), 0) + i * 8
        m = 64 * row - first - iota((8, Y), 1)
        phase_cos, phase_sin = unit(504 * m + row * off)
        top_cos, top_sin = unit(512 * m)
        low_cos, low_sin = unit(8 * m)
        same = (m & 4095) == 0
        ratio = jnp.where(
            same, top_cos * low_cos, top_sin / jnp.where(same, 1.0, 64.0 * low_sin)
        )
        at = pl.ds(pl.multiple_of(i * 8, 8), 8)
        g_tab[at, :Y] = phase_cos * ratio
        g_tab[at, Y:] = phase_sin * ratio
        return carry

    lax.fori_loop(0, S // 8, g_rows, 0)

    def mod_rows(i, carry):
        row = iota((8, Y), 0)
        v = jnp.zeros((8, Y), jnp.int32)
        for r in range(8):
            v = jnp.where(row == r, sub_v[facet_step(me, K - 1 - (i * 8 + r))], v)
        real, imag = unit(0 - v * (first + iota((8, Y), 1)))
        for h in range(2):
            mod[i * 2 + h, :, :Y] = real[h * 4 : h * 4 + 4]
            mod[i * 2 + h, :, Y:] = imag[h * 4 : h * 4 + 4]
        return carry

    lax.fori_loop(0, K // 8, mod_rows, 0)

    wide[:Y, :] = strips[...]
    wide[Y:, :X] = -strips[:, X:]
    wide[Y:, X:] = strips[:, :X]

    def a_copy(t):
        return pltpu.make_async_remote_copy(
            src_ref=part_out.at[t],
            dst_ref=part_in.at[t],
            send_sem=a_send.at[t],
            recv_sem=a_recv.at[t],
            device_id=(facet_step(me, K - 1 - t), col),
            device_id_type=MESH,
        )

    def facet_group(g, carry):
        for i in range(4):
            t = g * 4 + i
            for h in range(4):
                lanes = slice(h * X, (h + 1) * X)
                upper = slice(Y + h * X, Y + (h + 1) * X)
                gr = g_tab[:, lanes]
                gi = g_tab[:, upper]
                mr = mod[g, i : i + 1, lanes]
                mi = mod[g, i : i + 1, upper]
                m_tab[t, :, lanes] = (gr * mr - gi * mi).astype(BF16)
                m_tab[t, :, upper] = (gr * mi + gi * mr).astype(BF16)
        made = jnp.dot(
            m_tab[pl.ds(g * 4, 4)].reshape(4 * S, 2 * Y),
            wide[...],
            preferred_element_type=F32,
        )
        part_out[pl.ds(g * 4, 4)] = made.astype(BF16).reshape(4, S, 2 * X)
        own_part[...] = made[3 * S :, :]

        @pl.when(g == 0)
        def _():
            pl.semaphore_wait(barrier, K - 1 + C - 1)

        for i in range(4):
            t = g * 4 + i

            @pl.when(t < K - 1)
            def _():
                a_copy(t).start()

        return carry

    lax.fori_loop(0, K // 4, facet_group, 0)

    frequency = sub_u[col]

    def w_block(b, carry):
        for h in range(2):
            x = iota((X // 2, X), 0) + h * (X // 2)
            u = iota((X // 2, X), 1) + b * X
            real, imag = unit(0 - 64 * x * (frequency + u))
            top = slice(h * (X // 2), (h + 1) * (X // 2))
            low = slice(X + h * (X // 2), X + (h + 1) * (X // 2))
            w_tab[b, top, :X] = real.astype(BF16)
            w_tab[b, top, X:] = imag.astype(BF16)
            w_tab[b, low, :X] = (-imag).astype(BF16)
            w_tab[b, low, X:] = real.astype(BF16)
        return carry

    lax.fori_loop(0, UB, w_block, 0)

    strip = jnp.zeros((C, X), jnp.int32)
    for c in range(C):
        strip = jnp.where(iota((C, X), 0) == c, strip_off[c], strip)

    def d_block(b, carry):
        real, imag = unit(0 - strip * (frequency + iota((C, X), 1) + b * X))
        d_tab[b, :, :X] = real
        d_tab[b, :, X:] = imag
        return carry

    lax.fori_loop(0, UB, d_block, 0)

    row = iota((S, X), 0)
    lane = iota((S, X), 1)
    covers = (bands[0:1, :] == (row >> 3).astype(F32)) & ((row & 7) == (lane & 7))
    spread = jnp.where(covers, jnp.broadcast_to(bands[1:2, :], (S, X)), 0.0)
    weight[...] = jnp.broadcast_to(jnp.sum(spread, axis=1, keepdims=True), (S, X)) * (1.0 / 32.0)
    high = spread.astype(BF16)
    rest = (spread - high.astype(F32)).astype(BF16)
    both = jnp.concatenate([high, rest], axis=0)
    screen_load.wait()
    vis_load.wait()

    def base_block(b, carry):
        lanes = pl.ds(pl.multiple_of(b * X, X), X)
        upper = pl.ds(pl.multiple_of(U + b * X, X), X)
        real = jnp.dot(both, vis[:, lanes], preferred_element_type=F32)
        imag = jnp.dot(both, vis[:, upper], preferred_element_type=F32)
        real = real[:S] + real[S:]
        imag = imag[:S] + imag[S:]
        cos, sin = cos_sin(screen[:, lanes])
        base[b, :, :X] = real * cos + imag * sin
        base[b, :, X:] = imag * cos - real * sin
        return carry

    lax.fori_loop(0, UB, base_block, 0)

    def a_sum(t, total):
        a_copy(t).wait_recv()
        return total + part_in[t].astype(F32)

    total = lax.fori_loop(0, K - 1, a_sum, own_part[...])
    asm[col] = (total * (1.0 / 16.0)).astype(BF16)

    def c_copy(slot, q):
        return pltpu.make_async_remote_copy(
            src_ref=asm.at[slot],
            dst_ref=asm.at[slot],
            send_sem=c_send.at[q],
            recv_sem=c_recv.at[slot],
            device_id=(me, col_step(col, q)),
            device_id_type=MESH,
        )

    def c_start(q, carry):
        c_copy(col, q).start()
        return carry

    def c_wait(q, carry):
        c_copy(col_step(col, q), q).wait_recv()
        return carry

    lax.fori_loop(1, C, c_start, 0)
    lax.fori_loop(1, C, c_wait, 0)

    share_acc[...] = jnp.zeros_like(share_acc)

    def grid_block(b, carry):
        made = jnp.dot(asm[...].reshape(C * S, 2 * X), w_tab[b], preferred_element_type=F32)
        real = jnp.zeros((S, X), F32)
        imag = jnp.zeros((S, X), F32)
        for c in range(C):
            dr = d_tab[b, c : c + 1, :X]
            di = d_tab[b, c : c + 1, X:]
            pr = made[c * S : (c + 1) * S, :X]
            pi = made[c * S : (c + 1) * S, X:]
            real = real + (pr * dr - pi * di)
            imag = imag + (pr * di + pi * dr)
        real = base[b, :, :X] - weight[...] * real
        imag = base[b, :, X:] - weight[...] * imag
        lanes = pl.ds(pl.multiple_of(b * X, X), X)
        upper = pl.ds(pl.multiple_of(U + b * X, X), X)
        residual[:, lanes] = real.astype(BF16)
        residual[:, upper] = imag.astype(BF16)
        turned = []
        for c in range(C):
            dr = d_tab[b, c : c + 1, :X]
            di = d_tab[b, c : c + 1, X:]
            turned.append(
                jnp.concatenate(
                    [
                        (real * dr + imag * di).astype(BF16),
                        (imag * dr - real * di).astype(BF16),
                    ],
                    axis=1,
                )
            )
        share_acc[...] += lax.dot_general(
            jnp.concatenate(turned, axis=0),
            w_tab[b],
            (((1,), (1,)), ((), ())),
            preferred_element_type=F32,
        )
        return carry

    lax.fori_loop(0, UB, grid_block, 0)
    share_out[...] = share_acc[...].astype(BF16).reshape(C, S, 2 * X)

    def e_copy(slot, q):
        there = col_step(col, q)
        return pltpu.make_async_remote_copy(
            src_ref=share_out.at[there],
            dst_ref=share_in.at[slot],
            send_sem=e_send.at[q],
            recv_sem=e_recv.at[slot],
            device_id=(me, there),
            device_id_type=MESH,
        )

    def e_start(q, carry):
        e_copy(col, q).start()
        return carry

    def e_sum(q, total):
        there = col_step(col, q)
        e_copy(there, q).wait_recv()
        return total + share_in[there].astype(F32)

    lax.fori_loop(1, C, e_start, 0)
    own = share_acc[pl.ds(pl.multiple_of(col * S, S), S), :]
    total = lax.fori_loop(1, C, e_sum, own)
    share[...] = total.astype(BF16)

    def f_copy(t):
        p = K - 1 - t
        slot = K - 1 - back_step(p)
        return pltpu.make_async_remote_copy(
            src_ref=share,
            dst_ref=back.at[slot],
            send_sem=f_send.at[t],
            recv_sem=f_recv.at[slot],
            device_id=(facet_step(me, p), col),
            device_id_type=MESH,
        )

    def f_start(t, carry):
        f_copy(t).start()
        return carry

    lax.fori_loop(0, K - 1, f_start, 0)
    back[K - 1] = share[...]
    back_acc[...] = jnp.zeros_like(back_acc)

    def image_group(g, carry):
        slots = (K - 1 - back_step(K - 1 - g * 4)) // 4
        for i in range(4):
            t = slots * 4 + i

            @pl.when(t < K - 1)
            def _():
                pltpu.make_async_remote_copy(
                    src_ref=share,
                    dst_ref=back.at[t],
                    send_sem=f_send.at[t],
                    recv_sem=f_recv.at[t],
                    device_id=(me, col),
                    device_id_type=MESH,
                ).wait_recv()

        back_acc[...] += lax.dot_general(
            back[pl.ds(slots * 4, 4)].reshape(4 * S, 2 * X),
            m_tab[pl.ds(slots * 4, 4)].reshape(4 * S, 2 * Y),
            (((0,), (0,)), ((), ())),
            preferred_element_type=F32,
        )
        return carry

    lax.fori_loop(0, K // 4, image_group, 0)
    real = back_acc[:X, :Y] + back_acc[X:, Y:]
    imag = back_acc[X:, :Y] - back_acc[:X, Y:]
    image[:, :X] = (real.T * (1.0 / 512.0)).astype(BF16)
    image[:, X:] = (imag.T * (1.0 / 512.0)).astype(BF16)

    def sent(t, carry):
        a_copy(t).wait_send()
        f_copy(t).wait_send()
        return carry

    def sent_col(q, carry):
        c_copy(col, q).wait_send()
        e_copy(col, q).wait_send()
        return carry

    lax.fori_loop(0, K - 1, sent, 0)
    lax.fori_loop(1, C, sent_col, 0)


def shards(
    facet_strips,
    facet_off,
    strip_off,
    sub_v,
    sub_u,
    screen_phase,
    visibilities,
    block_band,
    vis_weight,
):
    bands = jnp.stack(
        [
            jnp.repeat(block_band[:, 0].astype(F32), 8),
            vis_weight.reshape(BLOCKS * 8),
        ]
    )
    smem = pl.BlockSpec(memory_space=pltpu.SMEM)
    vmem = pl.BlockSpec(memory_space=pltpu.VMEM)
    anywhere = pl.BlockSpec(memory_space=pl.ANY)
    dma = pltpu.SemaphoreType.DMA
    residual, image = pl.pallas_call(
        kernel,
        name="imaging_round",
        out_shape=(
            jax.ShapeDtypeStruct((S, 2 * U), BF16),
            jax.ShapeDtypeStruct((Y, 2 * X), BF16),
        ),
        in_specs=[smem] * 4 + [vmem] * 2 + [anywhere] * 2,
        out_specs=(vmem, vmem),
        scratch_shapes=[
            pltpu.VMEM((S, 2 * Y), F32),
            pltpu.VMEM((K // 4, 4, 2 * Y), F32),
            pltpu.VMEM((2 * Y, 2 * X), BF16),
            pltpu.VMEM((K, S, 2 * Y), BF16),
            pltpu.VMEM((K, S, 2 * X), BF16),
            pltpu.VMEM((K, S, 2 * X), BF16),
            pltpu.VMEM((S, 2 * X), F32),
            pltpu.VMEM((C, S, 2 * X), BF16),
            pltpu.VMEM((UB, 2 * X, 2 * X), BF16),
            pltpu.VMEM((UB, C, 2 * X), F32),
            pltpu.VMEM((S, U), F32),
            pltpu.VMEM((BLOCKS * 8, 2 * U), BF16),
            pltpu.VMEM((UB, S, 2 * X), F32),
            pltpu.VMEM((S, X), F32),
            pltpu.VMEM((C * S, 2 * X), F32),
            pltpu.VMEM((C, S, 2 * X), BF16),
            pltpu.VMEM((C, S, 2 * X), BF16),
            pltpu.VMEM((S, 2 * X), BF16),
            pltpu.VMEM((K, S, 2 * X), BF16),
            pltpu.VMEM((2 * X, 2 * Y), F32),
            dma((2,)),
            dma((K,)),
            dma((K,)),
            dma((C,)),
            dma((C,)),
            dma((C,)),
            dma((C,)),
            dma((K,)),
            dma((K,)),
        ],
        compiler_params=pltpu.CompilerParams(
            collective_id=0, has_side_effects=True, vmem_limit_bytes=48 * 1024 * 1024
        ),
    )(
        facet_off,
        strip_off,
        sub_v,
        sub_u,
        facet_strips.reshape(Y, 2 * X),
        bands,
        screen_phase,
        visibilities.reshape(BLOCKS * 8, 2 * U),
    )
    return residual.reshape(S, 2, U), image.reshape(Y, 2, X)


def solution(mesh):
    return jax.shard_map(
        shards,
        mesh=mesh,
        in_specs=(
            P("facet", None, "col"),
            P(),
            P(),
            P(),
            P(),
            P("facet", "col"),
            P("facet", None, None, "col"),
            P("facet", "col"),
            P("facet", "col"),
        ),
        out_specs=(P("facet", None, "col"), P("facet", None, "col")),
        check_vma=False,
    )
```

profile of v0, /device:TPU:1, one launch (start us, length us, event | category | flops | bytes accessed | tf_op | source)
XLA Modules:
  0.0 71.4 jit_solution(11417979477152921626)
XLA Ops:
  0.6 0.0 copy-start.6
  0.6 0.0 copy-start.5
  0.6 0.6 copy-done.6
  1.3 0.1 broadcast_in_dim.3
  1.4 0.1 stack_reshape.6
  1.5 0.8 %copy.12 = f32[16,8]{1,0:T(8,128)S(1)} copy(f32[16,8]{0,1:T(8,128)} %param.17) | data formatting | bytes 1024 | tf_op args[8]
  2.2 0.1 stack_reshape.7
  2.3 1.0 %copy.16 = bf16[64,8,2,128]{3,1,2,0:T(8,128)(2,1)S(1)} copy(bf16[64,8,2,128]{3,2,1,0:T(2,128)(2,1)} %bitcast.11) | data formatting | bytes 524288
  3.3 0.0 copy-done.5
  3.3 0.0 copy-start
  3.3 0.0 copy-start.4
  3.3 0.1 copy.14
  3.5 0.0 copy-start.1
  3.5 0.0 copy-start.2
  3.5 0.0 copy-start.3
  3.5 0.8 %copy-done = f32[64,1024]{1,0:T(8,128)S(1)} copy-done((f32[64,1024]{1,0:T(8,128)S(1)}, f32[64,1024]{1,0:T(8,128)}, u32[]{:S(2)}) %copy-start) | copy-done | bytes 262168
  4.3 0.0 copy-done.4
  4.3 0.0 copy-done.1
  4.3 0.0 copy-done.2
  4.3 0.0 copy-done.3
  4.3 65.5 %imaging_round.1 = (bf16[64,2048]{1,0:T(8,128)(2,1)S(1)}, bf16[512,256]{1,0:T(8,128)(2,1)S(1)}) custom-call(s32[4]{0:T(128)S(1)} %copy-done.1, s32[8]{0:T(128)S(1)} %copy-done.2, s32[32]{0:T(128)S(1)} %copy-done.3, s32[8]{0:T(128)S(1)} %copy-done.4, bf16[512,256]{1,0:T(8,128)(2,1)S(1)} %bitcast.10, f32[2,128]{1,0:T(2,128)S(1)} %pad_maximum_fusion.bands, ...), custom_call_target="tpu_custom_call" | custom-call | tf_op jit(solution)/shard_map/imaging_round/pallas_call | solution.py:461
  69.8 0.9 %reshape.19 = bf16[64,2,1024]{2,1,0:T(2,128)(2,1)} reshape(bf16[64,2048]{1,0:T(8,128)(2,1)S(1)} %get-tuple-element.4) | data formatting | bytes 524288 | tf_op jit(solution)/shard_map/reshape | solution.py:514
  70.7 0.8 %reshape.20 = bf16[512,2,128]{2,1,0:T(2,128)(2,1)} reshape(bf16[512,256]{1,0:T(8,128)(2,1)S(1)} %get-tuple-element.5) | data formatting | bytes 524288 | tf_op jit(solution)/shard_map/reshape | solution.py:514
  (2 shorter events, 0.0 us)
Async XLA Ops:
  0.6 0.7 copy-start.6
  0.6 2.7 %copy-start.5 = (bf16[16,8,2,1024]{3,2,1,0:T(2,128)(2,1)S(1)}, bf16[16,8,2,1024]{3,2,1,0:T(2,128)(2,1)}, u32[]{:S(2)}) copy-start(bf16[16,8,2,1024]{3,2,1,0:T(2,128)(2,1)} %param.15) | copy-start | bytes 1572868
  3.3 1.0 %copy-start = (f32[64,1024]{1,0:T(8,128)S(1)}, f32[64,1024]{1,0:T(8,128)}, u32[]{:S(2)}) copy-start(f32[64,1024]{1,0:T(8,128)} %screen_hbm.1) | copy-start | bytes 786436
  3.3 0.9 %copy-start.4 = (s32[8]{0:T(128)S(1)}, s32[8]{0:T(128)}, u32[]{:S(2)}) copy-start(s32[8]{0:T(128)} %sub_u.1) | copy-start | bytes 100
  3.5 0.8 %copy-start.1 = (s32[4]{0:T(128)S(1)}, s32[4]{0:T(128)}, u32[]{:S(2)}) copy-start(s32[4]{0:T(128)} %facet_off.1) | copy-start | bytes 52
  3.5 0.8 %copy-start.2 = (s32[8]{0:T(128)S(1)}, s32[8]{0:T(128)}, u32[]{:S(2)}) copy-start(s32[8]{0:T(128)} %strip_off.1) | copy-start | bytes 100
  3.5 0.8 %copy-start.3 = (s32[32]{0:T(128)S(1)}, s32[32]{0:T(128)}, u32[]{:S(2)}) copy-start(s32[32]{0:T(128)} %sub_v.1) | copy-start | bytes 388
where the time goes:
time: 71.8 us; the launch traced here: 71.4 us
  Pallas kernels  65.5 us (91%)
  local copies, waits for them, and re-layouts  5.2 us (7%)
  between operations  0.73 us (1%)
    pallas_call x1, Pallas kernels, shards(): pl.pallas_call(kernel, name='imaging_round', out_shape=(jax.ShapeDtypeStr...  65.5 us
    unnamed x17, local copies, waits for them, and re-layouts  3.31 us
    reshape x2, local copies, waits for them, and re-layouts, shards(): return (residual.reshape(S, 2, U), image.reshape(Y, 2, X))  1.65 us

commit v1 on v0

v1 whole, which is shorter than its diff:
```python
import math

import jax
import jax.numpy as jnp
from jax import lax
from jax.experimental import pallas as pl
from jax.experimental.pallas import tpu as pltpu
import numpy as np
from jax.sharding import PartitionSpec as P

MESH = pl.DeviceIdType.MESH
IMG = 65536
TURN = 2.0 * math.pi / IMG
F32 = jnp.float32
BF16 = jnp.bfloat16

K = 32
C = 8
S = 64
Y = 512
X = 128
U = 1024
PIECES = 8
UB = U // X
BLOCKS = 16
HALF = 12
TERMS = 2 * HALF
ROWS = 2 * TERMS
PIECE_COLS = PIECES * ROWS


def piece_factors():
    r = np.arange(S) - (S - 1) / 2
    d = np.arange(Y) - (Y - 1) / 2
    angle = 2.0 * np.pi * np.outer(r, d) / (PIECES * Y)
    left = []
    right = []
    for part in (np.cos(angle), np.sin(angle)):
        u, sigma, v = np.linalg.svd(part, full_matrices=False)
        left.append(u[:, :HALF] * sigma[:HALF])
        right.append(v[:HALF])
    q = np.concatenate(left, axis=1) / 1024.0
    b = np.concatenate(right, axis=0)
    return (
        np.tile(q, (1, 2 * PIECES)).astype(np.float32),
        np.repeat(b, 2, axis=1).astype(np.float32),
    )


def quarter_turns(q, t):
    t2 = t * t
    sin = t + t * t2 * (-1.6666654611e-1 + t2 * (8.3321608736e-3 + t2 * -1.9515295891e-4))
    cos = 1.0 - 0.5 * t2 + t2 * t2 * (
        4.166664568298827e-2 + t2 * (-1.388731625493765e-3 + t2 * 2.443315711809948e-5)
    )
    odd = (q & 1) == 1
    even_cos = jnp.where(odd, sin, cos)
    even_sin = jnp.where(odd, cos, sin)
    return (
        jnp.where(((q + 1) & 2) != 0, -even_cos, even_cos),
        jnp.where((q & 2) != 0, -even_sin, even_sin),
    )


def unit(k):
    k = k & (IMG - 1)
    q = (k + IMG // 8) >> 14
    return quarter_turns(q, (k - (q << 14)).astype(F32) * TURN)


def cos_sin(angle):
    turns = jnp.floor(angle * (2.0 / math.pi) + 0.5)
    t = (angle - turns * 1.5703125) - turns * 4.837512969970703e-4
    t = t - turns * 7.549789948768648e-8
    return quarter_turns(turns.astype(jnp.int32), t)


def iota(shape, dim):
    return lax.broadcasted_iota(jnp.int32, shape, dim)


def facet_step(me, p):
    x = ((me >> 3) + (p >> 3)) & 3
    z = ((me >> 2) ^ (p >> 2)) & 1
    y = (me + p) & 3
    return (x << 3) | (z << 2) | y


def back_step(p):
    x = (0 - (p >> 3)) & 3
    y = (0 - p) & 3
    return (x << 3) | (p & 4) | y


def kernel(
    facet_off_hbm,
    strip_off_hbm,
    sub_v_hbm,
    sub_u_hbm,
    strips_hbm,
    b_hbm,
    q_hbm,
    band_hbm,
    weight_hbm,
    screen_hbm,
    vis_hbm,
    residual,
    image,
    facet_off,
    strip_off,
    sub_v,
    sub_u,
    band,
    row_weight,
    strips,
    b_tab,
    q_tab,
    screen,
    vis,
    mod,
    n_tab,
    part_out,
    part_in,
    l_tab,
    lt_tab,
    asm,
    w_tab,
    d_tab,
    base,
    weight,
    rest,
    rest_out,
    share_acc,
    pair_out,
    pair_in,
    share_out,
    share_in,
    back_out,
    back,
    back_acc,
    load_sem,
    vis_sem,
    rest_sem,
    a_send,
    a_recv,
    c_send,
    c_recv,
    pair_send,
    pair_recv,
    e_send,
    e_recv,
    f_send,
    f_recv,
):
    me = lax.axis_index("facet")
    col = lax.axis_index("col")
    z = col >> 1
    core = col & 1
    sibling = 1 - core

    loads = [
        pltpu.make_async_copy(src, dst, load_sem.at[i])
        for i, (src, dst) in enumerate(
            [
                (facet_off_hbm, facet_off),
                (sub_v_hbm, sub_v),
                (b_hbm, b_tab),
                (strips_hbm, strips),
                (strip_off_hbm, strip_off),
                (sub_u_hbm, sub_u),
                (band_hbm, band),
                (weight_hbm, row_weight),
                (q_hbm, q_tab),
                (screen_hbm, screen),
            ]
        )
    ]
    for load in loads:
        load.start()
    barrier = pltpu.get_barrier_semaphore()

    def greet_facet(p, carry):
        pl.semaphore_signal(
            barrier, inc=1, device_id=(facet_step(me, p), col), device_id_type=MESH
        )
        return carry

    lax.fori_loop(1, K, greet_facet, 0)
    for other in [2 * z + sibling] + [2 * ((z + dz) & 3) + core for dz in (1, 2, 3)]:
        pl.semaphore_signal(barrier, inc=1, device_id=(me, other), device_id_type=MESH)

    def vis_load(b):
        lanes = pl.ds(pl.multiple_of(b * X, X), X)
        return pltpu.make_async_copy(vis_hbm.at[:, :, lanes], vis.at[b], vis_sem.at[b])

    def vis_start(b, carry):
        vis_load(b).start()
        return carry

    lax.fori_loop(0, UB, vis_start, 0)

    for load in loads[:4]:
        load.wait()
    first = facet_off[me // PIECES] + (me % PIECES) * Y

    def mod_rows(i, carry):
        row = iota((8, X), 0)
        v = jnp.zeros((8, X), jnp.int32)
        for r in range(8):
            v = jnp.where(row == r, sub_v[i * 8 + r], v)
        for h in range(2 * Y // X):
            lane = iota((8, X), 1) + h * X
            y = lane >> 1
            real, imag = unit(128772 - 504 * y - v * (first + y) + ((lane & 1) << 14))
            for g in range(2):
                mod[i * 2 + g, :, h * X : (h + 1) * X] = real[g * 4 : g * 4 + 4]
                mod[i * 2 + g, :, 2 * Y + h * X : 2 * Y + (h + 1) * X] = imag[g * 4 : g * 4 + 4]
        return carry

    lax.fori_loop(0, K // 8, mod_rows, 0)

    def facet_group(g, carry):
        for h in range(2 * Y // X):
            lanes = slice(h * X, (h + 1) * X)
            upper = slice(2 * Y + h * X, 2 * Y + (h + 1) * X)
            b = b_tab[:, lanes]
            for i in range(4):
                n_tab[g * 4 + i, :, lanes] = jnp.concatenate(
                    [b * mod[g, i : i + 1, lanes], b * mod[g, i : i + 1, upper]], axis=0
                ).astype(BF16)
        made = jnp.dot(
            n_tab[pl.ds(g * 4, 4)].reshape(4 * ROWS, 2 * Y),
            strips[...],
            preferred_element_type=F32,
        )
        part_out[pl.ds(g * 4, 4)] = made.astype(BF16).reshape(4, ROWS, X)
        return carry

    lax.fori_loop(0, K // 4, facet_group, 0)
    pl.semaphore_wait(barrier, K - 1 + 4)

    def a_copy(p):
        there = facet_step(me, p)
        return pltpu.make_async_remote_copy(
            src_ref=part_out.at[there],
            dst_ref=part_in.at[me],
            send_sem=a_send.at[p],
            recv_sem=a_recv.at[me],
            device_id=(there, col),
            device_id_type=MESH,
        )

    def a_arrival(p):
        source = facet_step(me, back_step(p))
        return pltpu.make_async_remote_copy(
            src_ref=part_out.at[source],
            dst_ref=part_in.at[source],
            send_sem=a_send.at[p],
            recv_sem=a_recv.at[source],
            device_id=(source, col),
            device_id_type=MESH,
        )

    def a_start(i, carry):
        a_copy(K - 1 - i).start()
        return carry

    lax.fori_loop(0, K - 1, a_start, 0)
    part_in[me] = part_out[me]

    for load in loads[4:]:
        load.wait()

    l_lane = iota((8, PIECE_COLS), 1)
    piece = jnp.zeros((8, PIECE_COLS), jnp.int32)
    for h in range(1, PIECES):
        piece = piece + (l_lane >= h * ROWS).astype(jnp.int32)
    l_term = l_lane - piece * ROWS
    l_imag = (l_term >= TERMS).astype(jnp.int32)
    l_odd = (l_term - l_imag * TERMS >= HALF).astype(jnp.int32)
    l_quarter = ((l_imag - l_odd) << 14)[0:1]
    l_place = (piece * (16 * Y) + 4088)[0:1]

    def l_facet(f, carry):
        off = facet_off[f]
        r = iota((S, PIECE_COLS), 0)
        real, imag = unit(l_quarter - r * (16 * off + l_place))
        q = q_tab[...]
        right = jnp.concatenate([q * real, q * imag], axis=0)
        row = iota((2 * S, 2 * S), 0)
        lane = iota((2 * S, 2 * S), 1)
        left, _ = unit(
            (row & (S - 1)) * (off + 1024 * (lane & (S - 1))) + (((lane >> 6) - (row >> 6)) << 14)
        )
        made = jnp.dot(left, right, precision=lax.Precision.HIGHEST, preferred_element_type=F32)
        l_tab[:, pl.ds(pl.multiple_of(f * PIECE_COLS, X), PIECE_COLS)] = made.astype(BF16)
        lt_tab[f] = made.T.astype(BF16)
        return carry

    lax.fori_loop(0, 4, l_facet, 0)
    frequency = sub_u[col]

    def w_block(b, carry):
        for h in range(2):
            x = iota((X // 2, X), 0) + h * (X // 2)
            u = iota((X // 2, X), 1) + b * X
            real, imag = unit(0 - 64 * x * (frequency + u))
            top = slice(h * (X // 2), (h + 1) * (X // 2))
            low = slice(X + h * (X // 2), X + (h + 1) * (X // 2))
            w_tab[b, top, :X] = real.astype(BF16)
            w_tab[b, top, X:] = imag.astype(BF16)
            w_tab[b, low, :X] = (-imag).astype(BF16)
            w_tab[b, low, X:] = real.astype(BF16)
        return carry

    lax.fori_loop(0, UB, w_block, 0)

    strip = jnp.zeros((C, X), jnp.int32)
    for c in range(C):
        strip = jnp.where(iota((C, X), 0) == (c & 1) * 4 + (c >> 1), strip_off[c], strip)

    def d_block(b, carry):
        real, imag = unit(0 - strip * (frequency + iota((C, X), 1) + b * X))
        for h in range(2):
            d_tab[h, b, :, :X] = real[h * 4 : h * 4 + 4]
            d_tab[h, b, :, X:] = imag[h * 4 : h * 4 + 4]
        return carry

    lax.fori_loop(0, UB, d_block, 0)

    pair_lane = iota((8, 2 * X), 1) >> 1

    def weight_lane(i, total):
        return jnp.where(pair_lane == i, row_weight[i >> 3, i & 7], total)

    weight_row = lax.fori_loop(0, BLOCKS * 8, weight_lane, jnp.zeros((8, 2 * X), F32))
    band_row = jnp.zeros((8, 2 * X), jnp.int32)
    for b in range(BLOCKS):
        band_row = jnp.where((pair_lane >> 3) == b, band[b, 0], band_row)
    row = iota((2 * S, 2 * X), 0)
    lane = iota((2 * S, 2 * X), 1)
    covers = (
        (band_row[0:1] == ((row & (S - 1)) >> 3))
        & (((lane >> 1) & 7) == (row & 7))
        & ((lane & 1) == (row >> 6))
    )
    spread = jnp.where(covers, jnp.broadcast_to(weight_row[0:1], (2 * S, 2 * X)), 0.0)
    weight[...] = jnp.broadcast_to(jnp.sum(spread[:S], axis=1, keepdims=True), (S, X)) * (
        1.0 / 32.0
    )
    high = spread.astype(BF16)
    both = jnp.concatenate([high, (spread - high.astype(F32)).astype(BF16)], axis=0)

    def base_block(b, carry):
        vis_load(b).wait()
        made = jnp.dot(both, vis.at[b].reshape(2 * X, X)[...], preferred_element_type=F32)
        real = made[:S] + made[2 * S : 3 * S]
        imag = made[S : 2 * S] + made[3 * S :]
        cos, sin = cos_sin(screen[:, pl.ds(pl.multiple_of(b * X, X), X)])
        base[b, :, :X] = real * cos + imag * sin
        base[b, :, X:] = imag * cos - real * sin
        return carry

    lax.fori_loop(0, UB, base_block, 0)

    def a_wait(i, carry):
        a_arrival(K - 1 - i).wait_recv()
        return carry

    lax.fori_loop(0, K - 1, a_wait, 0)
    made = jnp.dot(l_tab[...], part_in[...].reshape(K * ROWS, X), preferred_element_type=F32)
    asm[core * 4 + z] = jnp.concatenate([made[:S], made[S:]], axis=1).astype(BF16)

    def c_copy(slot, send, there):
        return pltpu.make_async_remote_copy(
            src_ref=asm.at[slot],
            dst_ref=asm.at[slot],
            send_sem=c_send.at[send],
            recv_sem=c_recv.at[slot],
            device_id=(me, there),
            device_id_type=MESH,
        )

    c_copies = [
        c_copy(core * 4 + z, dz, 2 * ((z + dz) & 3) + core) for dz in (2, 1, 3)
    ] + [c_copy(core * 4 + z, 0, 2 * z + sibling)]
    for copy in c_copies:
        copy.start()
    for dz in (1, 3, 2):
        slot = core * 4 + ((z - dz) & 3)
        c_copy(slot, dz, 2 * ((z - dz) & 3) + core).wait_recv()
        forward = c_copy(slot, 3 + dz, 2 * z + sibling)
        forward.start()
        c_copies.append(forward)
    for other in range(4):
        c_copy(sibling * 4 + other, 0, 2 * z + sibling).wait_recv()

    row = iota((2 * S, 2 * S), 0)
    lane = iota((2 * S, 2 * S), 1)
    weave = ((row >> 1) == (lane & (S - 1))) & ((row & 1) == (lane >> 6))
    weave = jnp.where(weave, 1.0, 0.0).astype(BF16)

    def rest_store(b):
        lanes = pl.ds(pl.multiple_of(b * X, X), X)
        return pltpu.make_async_copy(rest_out.at[b], residual.at[:, :, lanes], rest_sem.at[b])

    def grid_block(b, carry):
        made = jnp.dot(asm[...].reshape(C * S, 2 * X), w_tab[b], preferred_element_type=F32)
        real = jnp.zeros((S, X), F32)
        imag = jnp.zeros((S, X), F32)
        for c in range(C):
            dr = d_tab[c // 4, b, c % 4 : c % 4 + 1, :X]
            di = d_tab[c // 4, b, c % 4 : c % 4 + 1, X:]
            pr = made[c * S : (c + 1) * S, :X]
            pi = made[c * S : (c + 1) * S, X:]
            real = real + (pr * dr - pi * di)
            imag = imag + (pr * di + pi * dr)
        real = base[b, :, :X] - weight[...] * real
        imag = base[b, :, X:] - weight[...] * imag
        rest[b, :, :X] = real
        rest[b, :, X:] = imag
        woven = jnp.dot(
            weave,
            jnp.concatenate([real, imag], axis=0).astype(BF16),
            preferred_element_type=F32,
        )
        rest_out.at[b].reshape(2 * S, X)[...] = woven.astype(BF16)
        rest_store(b).start()
        return carry

    lax.fori_loop(0, UB, grid_block, 0)

    def share_of(parity):
        share_acc[...] = jnp.zeros_like(share_acc)

        def share_block(b, carry):
            real = rest[b, :, :X]
            imag = rest[b, :, X:]
            turned = []
            for c in range(4):
                dr = d_tab[parity, b, c : c + 1, :X]
                di = d_tab[parity, b, c : c + 1, X:]
                turned.append(
                    jnp.concatenate(
                        [
                            (real * dr + imag * di).astype(BF16),
                            (imag * dr - real * di).astype(BF16),
                        ],
                        axis=1,
                    )
                )
            share_acc[...] += lax.dot_general(
                jnp.concatenate(turned, axis=0),
                w_tab[b],
                (((1,), (1,)), ((), ())),
                preferred_element_type=F32,
            )
            return carry

        lax.fori_loop(0, UB, share_block, 0)

    share_of(sibling)
    pair_out[...] = share_acc[...].astype(BF16).reshape(4, S, 2 * X)
    pair = pltpu.make_async_remote_copy(
        src_ref=pair_out,
        dst_ref=pair_in,
        send_sem=pair_send,
        recv_sem=pair_recv,
        device_id=(me, 2 * z + sibling),
        device_id_type=MESH,
    )
    pair.start()
    share_of(core)
    pair.wait_recv()

    def strip_total(at):
        rows = pl.ds(pl.multiple_of(at * S, S), S)
        return share_acc[rows, :] + pair_in[at].astype(F32)

    def e_copy(there, slot, dz):
        return pltpu.make_async_remote_copy(
            src_ref=share_out.at[there],
            dst_ref=share_in.at[slot],
            send_sem=e_send.at[dz],
            recv_sem=e_recv.at[slot],
            device_id=(me, 2 * there + core),
            device_id_type=MESH,
        )

    for dz in (2, 1, 3):
        there = (z + dz) & 3
        share_out[there] = strip_total(there).astype(BF16)
        e_copy(there, z, dz).start()
    total = strip_total(z)
    for dz in (1, 3, 2):
        there = (z - dz) & 3
        e_copy(there, there, dz).wait_recv()
        total = total + share_in[there].astype(F32)
    share = jnp.concatenate([total[:, :X], total[:, X:]], axis=0).astype(BF16)

    made = jnp.dot(lt_tab[...].reshape(K * ROWS, X), share, preferred_element_type=F32)
    back_out[...] = made.astype(BF16).reshape(K, ROWS, X)

    def f_copy(p):
        there = facet_step(me, p)
        return pltpu.make_async_remote_copy(
            src_ref=back_out.at[there],
            dst_ref=back.at[me],
            send_sem=f_send.at[p],
            recv_sem=f_recv.at[me],
            device_id=(there, col),
            device_id_type=MESH,
        )

    def f_arrival(p):
        source = facet_step(me, back_step(p))
        return pltpu.make_async_remote_copy(
            src_ref=back_out.at[source],
            dst_ref=back.at[source],
            send_sem=f_send.at[p],
            recv_sem=f_recv.at[source],
            device_id=(source, col),
            device_id_type=MESH,
        )

    def f_start(i, carry):
        f_copy(K - 1 - i).start()
        return carry

    lax.fori_loop(0, K - 1, f_start, 0)
    back[me] = back_out[me]
    back_acc[...] = jnp.zeros_like(back_acc)

    def image_group(i, carry):
        dx = 3 - i
        start = (((me >> 3) - dx) & 3) * 8

        def f_wait(j, inner):
            f_arrival(dx * 8 + j).wait_recv()
            return inner

        lax.fori_loop(jnp.where(dx == 0, 1, 0), 8, f_wait, 0)
        back_acc[...] += lax.dot_general(
            back[pl.ds(start, 8)].reshape(8 * ROWS, X),
            n_tab[pl.ds(start, 8)].reshape(8 * ROWS, 2 * Y),
            (((0,), (0,)), ((), ())),
            preferred_element_type=F32,
        )
        return carry

    lax.fori_loop(0, 4, image_group, 0)
    image[...] = (back_acc[...].T * (1.0 / 32.0)).astype(BF16)

    def sent(p, carry):
        a_copy(p).wait_send()
        f_copy(p).wait_send()
        return carry

    lax.fori_loop(1, K, sent, 0)
    for copy in c_copies:
        copy.wait_send()
    pair.wait_send()
    for dz in (2, 1, 3):
        e_copy((z + dz) & 3, z, dz).wait_send()

    def stored(b, carry):
        rest_store(b).wait()
        return carry

    lax.fori_loop(0, UB, stored, 0)


def shards(
    facet_strips,
    facet_off,
    strip_off,
    sub_v,
    sub_u,
    screen_phase,
    visibilities,
    block_band,
    vis_weight,
):
    vmem = pl.BlockSpec(memory_space=pltpu.VMEM)
    anywhere = pl.BlockSpec(memory_space=pl.ANY)
    dma = pltpu.SemaphoreType.DMA
    q, b = piece_factors()
    residual, image = pl.pallas_call(
        kernel,
        name="imaging_round",
        out_shape=(
            jax.ShapeDtypeStruct((S, 2, U), BF16),
            jax.ShapeDtypeStruct((2 * Y, X), BF16),
        ),
        in_specs=[anywhere] * 11,
        out_specs=(anywhere, vmem),
        scratch_shapes=[
            pltpu.SMEM((4,), jnp.int32),
            pltpu.SMEM((C,), jnp.int32),
            pltpu.SMEM((K,), jnp.int32),
            pltpu.SMEM((C,), jnp.int32),
            pltpu.SMEM((BLOCKS, 1), jnp.int32),
            pltpu.SMEM((BLOCKS, 8), F32),
            pltpu.VMEM((2 * Y, X), BF16),
            pltpu.VMEM((TERMS, 2 * Y), F32),
            pltpu.VMEM((S, PIECE_COLS), F32),
            pltpu.VMEM((S, U), F32),
            pltpu.VMEM((UB, BLOCKS * 8, 2, X), BF16),
            pltpu.VMEM((K // 4, 4, 4 * Y), F32),
            pltpu.VMEM((K, ROWS, 2 * Y), BF16),
            pltpu.VMEM((K, ROWS, X), BF16),
            pltpu.VMEM((K, ROWS, X), BF16),
            pltpu.VMEM((2 * S, K * ROWS), BF16),
            pltpu.VMEM((4, PIECE_COLS, 2 * S), BF16),
            pltpu.VMEM((C, S, 2 * X), BF16),
            pltpu.VMEM((UB, 2 * X, 2 * X), BF16),
            pltpu.VMEM((2, UB, 4, 2 * X), F32),
            pltpu.VMEM((UB, S, 2 * X), F32),
            pltpu.VMEM((S, X), F32),
            pltpu.VMEM((UB, S, 2 * X), F32),
            pltpu.VMEM((UB, S, 2, X), BF16),
            pltpu.VMEM((4 * S, 2 * X), F32),
            pltpu.VMEM((4, S, 2 * X), BF16),
            pltpu.VMEM((4, S, 2 * X), BF16),
            pltpu.VMEM((4, S, 2 * X), BF16),
            pltpu.VMEM((4, S, 2 * X), BF16),
            pltpu.VMEM((K, ROWS, X), BF16),
            pltpu.VMEM((K, ROWS, X), BF16),
            pltpu.VMEM((X, 2 * Y), F32),
            dma((10,)),
            dma((UB,)),
            dma((UB,)),
            dma((K,)),
            dma((K,)),
            dma((8,)),
            dma((C,)),
            dma,
            dma,
            dma((4,)),
            dma((4,)),
            dma((K,)),
            dma((K,)),
        ],
        compiler_params=pltpu.CompilerParams(
            collective_id=0, has_side_effects=True, vmem_limit_bytes=48 * 1024 * 1024
        ),
    )(
        facet_off,
        strip_off,
        sub_v,
        sub_u,
        facet_strips.reshape(2 * Y, X),
        jnp.asarray(b),
        jnp.asarray(q),
        block_band,
        vis_weight,
        screen_phase,
        visibilities.reshape(BLOCKS * 8, 2, U),
    )
    return residual, image.reshape(Y, 2, X)


def solution(mesh):
    return jax.shard_map(
        shards,
        mesh=mesh,
        in_specs=(
            P("facet", None, "col"),
            P(),
            P(),
            P(),
            P(),
            P("facet", "col"),
            P("facet", None, None, "col"),
            P("facet", "col"),
            P("facet", "col"),
        ),
        out_specs=(P("facet", None, "col"), P("facet", None, "col")),
        check_vma=False,
    )
```

time: 71.8 us -> 58.1 us (0.81)
  Pallas kernels: 65.5 us -> 49 us
  local copies, waits for them, and re-layouts: 5.2 us -> 8.16 us
    pallas_call x1, Pallas kernels: 65.5 us -> 49 us  [shards(): pl.pallas_call(kernel, name='imaging_round', out_shape=(jax.ShapeDtypeStr...]
    unnamed x17 -> x26, local copies, waits for them, and re-layouts: 3.31 us -> 8.16 us
    reshape x2 -> x0, local copies, waits for them, and re-layouts: 1.65 us -> none  [shards(): return (residual.reshape(S, 2, U), image.reshape(Y, 2, X))]
where the time goes in v1:
time: 58.1 us; the launch traced here: 57.8 us
  Pallas kernels  49 us (84%)
  local copies, waits for them, and re-layouts  8.16 us (14%)
  between operations  0.66 us (1%)
    pallas_call x1, Pallas kernels, shards(): pl.pallas_call(kernel, name='imaging_round', out_shape=(jax.ShapeDtypeStr...  49 us
    unnamed x26, local copies, waits for them, and re-layouts  8.16 us

profile of v1, /device:TPU:1, one launch (start us, length us, event | category | flops | bytes accessed | tf_op | source)
XLA Modules:
  0.0 57.8 jit_solution(1272275513127919051)
XLA Ops:
  0.6 0.0 copy-start.10
  0.6 0.6 %copy-done.10 = s32[16,1]{0,1:T(1,128)S(1)} copy-done((s32[16,1]{0,1:T(1,128)S(1)}, s32[16,1]{0,1:T(1,128)}, u32[]{:S(2)}) %copy-start.10) | copy-done | bytes 88
  1.3 0.0 copy-start.9
  1.3 0.1 copy.13.band_hbm
  1.4 0.6 %copy-done.9 = f32[16,8]{0,1:T(8,128)S(1)} copy-done((f32[16,8]{0,1:T(8,128)S(1)}, f32[16,8]{0,1:T(8,128)}, u32[]{:S(2)}) %copy-start.9) | copy-done | bytes 536
  2.0 0.0 copy-start.5
  2.0 0.0 copy-start.6
  2.0 0.0 copy-start.7
  2.0 0.0 copy-start.8
  2.0 0.1 copy.14.weight_hbm
  2.1 0.6 copy-done.5
  2.6 0.0 copy-done.6
  2.6 0.0 copy-done.7
  2.7 0.0 copy-done.8
  2.7 0.0 copy-start
  2.7 1.0 %copy-done = bf16[16,8,2,1024]{3,2,1,0:T(2,128)(2,1)S(1)} copy-done((bf16[16,8,2,1024]{3,2,1,0:T(2,128)(2,1)S(1)}, bf16[16,8,2,1024]{3,2,1,0:T(2,128)(2,1)}, u32[]{:S(2)}) %copy-start) | copy-done | bytes 524312
  3.7 0.0 copy-start.1
  3.7 0.9 %copy-done.1 = bf16[512,2,128]{2,1,0:T(2,128)(2,1)S(1)} copy-done((bf16[512,2,128]{2,1,0:T(2,128)(2,1)S(1)}, bf16[512,2,128]{2,1,0:T(2,128)(2,1)}, u32[]{:S(2)}) %copy-start.1) | copy-done | bytes 262168
  4.7 0.0 copy-start.2
  4.7 0.9 %copy-done.2 = f32[64,1024]{1,0:T(8,128)S(1)} copy-done((f32[64,1024]{1,0:T(8,128)S(1)}, f32[64,1024]{1,0:T(8,128)}, u32[]{:S(2)}) %copy-start.2) | copy-done | bytes 262168
  5.6 0.0 copy-start.3
  5.6 0.9 %copy-done.3 = f32[64,384]{1,0:T(8,128)S(1)} copy-done((f32[64,384]{1,0:T(8,128)S(1)}, f32[64,384]{1,0:T(8,128)}, u32[]{:S(2)}) %copy-start.3) | copy-done | bytes 98328
  6.5 0.0 copy-start.4
  6.5 0.9 %copy-done.4 = f32[24,1024]{1,0:T(8,128)S(1)} copy-done((f32[24,1024]{1,0:T(8,128)S(1)}, f32[24,1024]{1,0:T(8,128)}, u32[]{:S(2)}) %copy-start.4) | copy-done | bytes 98328
  7.4 49.0 %imaging_round.1 = (bf16[64,2,1024]{2,1,0:T(2,128)(2,1)S(1)}, bf16[1024,128]{1,0:T(8,128)(2,1)S(1)}) custom-call(s32[4]{0:T(128)S(1)} %copy-done.5, s32[8]{0:T(128)S(1)} %copy-done.6, s32[32]{0:T(128)S(1)} %copy-done.7, s32[8]{0:T(128)S(1)} %copy-done.8, bf16[1024,128]{1,0:T(8,128)(2,1)S(1)} %bitcast.4, f32[24,1024]{1,0:T(8,128)S(1)} %copy-done.4, ...), custom_call_target="tpu_custom_call" | custom-call | tf_op jit(solution)/shard_map/imaging_round/pallas_call | solution.py:588
  56.4 0.7 %copy.17 = bf16[64,2,1024]{2,1,0:T(2,128)(2,1)} copy(bf16[64,2,1024]{2,1,0:T(2,128)(2,1)S(1)} %get-tuple-element.8) | data formatting | bytes 524288
  57.1 0.7 %copy.18 = bf16[512,2,128]{2,1,0:T(2,128)(2,1)} copy(bf16[512,2,128]{2,1,0:T(2,128)(2,1)S(1)} %bitcast.5) | data formatting | bytes 524288
Async XLA Ops:
  0.6 0.7 %copy-start.10 = (s32[16,1]{0,1:T(1,128)S(1)}, s32[16,1]{0,1:T(1,128)}, u32[]{:S(2)}) copy-start(s32[16,1]{0,1:T(1,128)} %param.18) | copy-start | bytes 196
  1.3 0.7 %copy-start.9 = (f32[16,8]{0,1:T(8,128)S(1)}, f32[16,8]{0,1:T(8,128)}, u32[]{:S(2)}) copy-start(f32[16,8]{0,1:T(8,128)} %param.19) | copy-start | bytes 1540
  2.0 0.7 %copy-start.5 = (s32[4]{0:T(128)S(1)}, s32[4]{0:T(128)}, u32[]{:S(2)}) copy-start(s32[4]{0:T(128)} %facet_off_hbm.1) | copy-start | bytes 52
  2.0 0.7 %copy-start.6 = (s32[8]{0:T(128)S(1)}, s32[8]{0:T(128)}, u32[]{:S(2)}) copy-start(s32[8]{0:T(128)} %strip_off_hbm.1) | copy-start | bytes 100
  2.0 0.7 %copy-start.7 = (s32[32]{0:T(128)S(1)}, s32[32]{0:T(128)}, u32[]{:S(2)}) copy-start(s32[32]{0:T(128)} %sub_v_hbm.1) | copy-start | bytes 388
  2.0 0.7 %copy-start.8 = (s32[8]{0:T(128)S(1)}, s32[8]{0:T(128)}, u32[]{:S(2)}) copy-start(s32[8]{0:T(128)} %sub_u_hbm.1) | copy-start | bytes 100
  2.7 1.0 %copy-start = (bf16[16,8,2,1024]{3,2,1,0:T(2,128)(2,1)S(1)}, bf16[16,8,2,1024]{3,2,1,0:T(2,128)(2,1)}, u32[]{:S(2)}) copy-start(bf16[16,8,2,1024]{3,2,1,0:T(2,128)(2,1)} %param.17) | copy-start | bytes 1572868
  3.7 0.9 %copy-start.1 = (bf16[512,2,128]{2,1,0:T(2,128)(2,1)S(1)}, bf16[512,2,128]{2,1,0:T(2,128)(2,1)}, u32[]{:S(2)}) copy-start(bf16[512,2,128]{2,1,0:T(2,128)(2,1)} %param.11) | copy-start | bytes 786436
  4.7 0.9 %copy-start.2 = (f32[64,1024]{1,0:T(8,128)S(1)}, f32[64,1024]{1,0:T(8,128)}, u32[]{:S(2)}) copy-start(f32[64,1024]{1,0:T(8,128)} %screen_hbm.1) | copy-start | bytes 786436
  5.6 0.9 %copy-start.3 = (f32[64,384]{1,0:T(8,128)S(1)}, f32[64,384]{1,0:T(8,128)}, u32[]{:S(2)}) copy-start(f32[64,384]{1,0:T(8,128)} %constant.5.clone.q_hbm) | copy-start | bytes 294916
  6.5 0.9 %copy-start.4 = (f32[24,1024]{1,0:T(8,128)S(1)}, f32[24,1024]{1,0:T(8,128)}, u32[]{:S(2)}) copy-start(f32[24,1024]{1,0:T(8,128)} %constant.4.clone.b_hbm) | copy-start | bytes 294916

commit v2 on v1

--- a/solution.py
+++ b/solution.py
@@ -23,6 +23,7 @@
 PIECES = 8
 UB = U // X
 BLOCKS = 16
+PLACES = (0, 1, 3, 2)
 HALF = 12
 TERMS = 2 * HALF
 ROWS = 2 * TERMS
@@ -90,6 +91,12 @@
     x = (0 - (p >> 3)) & 3
     y = (0 - p) & 3
     return (x << 3) | (p & 4) | y
+
+
+def far_first(i):
+    a = i >> 3
+    b = i & 3
+    return ((2 ^ a ^ (a >> 1)) << 3) | (4 - (i & 4)) | (2 ^ b ^ (b >> 1))
 
 
 def kernel(
@@ -128,7 +135,6 @@
     d_tab,
     base,
     weight,
-    rest,
     rest_out,
     share_acc,
     pair_out,
@@ -175,19 +181,21 @@
             ]
         )
     ]
-    for load in loads:
+    for load in loads[:4]:
         load.start()
     barrier = pltpu.get_barrier_semaphore()
 
-    def greet_facet(p, carry):
+    def greet_facet(i, carry):
         pl.semaphore_signal(
-            barrier, inc=1, device_id=(facet_step(me, p), col), device_id_type=MESH
-        )
-        return carry
-
-    lax.fori_loop(1, K, greet_facet, 0)
+            barrier, inc=1, device_id=(facet_step(me, far_first(i)), col), device_id_type=MESH
+        )
+        return carry
+
+    lax.fori_loop(0, K - 1, greet_facet, 0)
     for other in [2 * z + sibling] + [2 * ((z + dz) & 3) + core for dz in (1, 2, 3)]:
         pl.semaphore_signal(barrier, inc=1, device_id=(me, other), device_id_type=MESH)
+    for load in loads[4:]:
+        load.start()
 
     def vis_load(b):
         lanes = pl.ds(pl.multiple_of(b * X, X), X)
@@ -262,7 +270,7 @@
         )
 
     def a_start(i, carry):
-        a_copy(K - 1 - i).start()
+        a_copy(far_first(i)).start()
         return carry
 
     lax.fori_loop(0, K - 1, a_start, 0)
@@ -316,14 +324,16 @@
     lax.fori_loop(0, UB, w_block, 0)
 
     strip = jnp.zeros((C, X), jnp.int32)
-    for c in range(C):
-        strip = jnp.where(iota((C, X), 0) == (c & 1) * 4 + (c >> 1), strip_off[c], strip)
+    for at, step in enumerate(PLACES):
+        for c in range(2):
+            strip = jnp.where(
+                iota((C, X), 0) == 2 * at + c, strip_off[2 * ((z + step) & 3) + c], strip
+            )
 
     def d_block(b, carry):
         real, imag = unit(0 - strip * (frequency + iota((C, X), 1) + b * X))
-        for h in range(2):
-            d_tab[h, b, :, :X] = real[h * 4 : h * 4 + 4]
-            d_tab[h, b, :, X:] = imag[h * 4 : h * 4 + 4]
+        d_tab[b, :, :X] = real
+        d_tab[b, :, X:] = imag
         return carry
 
     lax.fori_loop(0, UB, d_block, 0)
@@ -331,12 +341,12 @@
     pair_lane = iota((8, 2 * X), 1) >> 1
 
     def weight_lane(i, total):
-        return jnp.where(pair_lane == i, row_weight[i >> 3, i & 7], total)
+        return jnp.where(pair_lane == i, row_weight[i & 7, i >> 3], total)
 
     weight_row = lax.fori_loop(0, BLOCKS * 8, weight_lane, jnp.zeros((8, 2 * X), F32))
     band_row = jnp.zeros((8, 2 * X), jnp.int32)
     for b in range(BLOCKS):
-        band_row = jnp.where((pair_lane >> 3) == b, band[b, 0], band_row)
+        band_row = jnp.where((pair_lane >> 3) == b, band[0, b], band_row)
     row = iota((2 * S, 2 * X), 0)
     lane = iota((2 * S, 2 * X), 1)
     covers = (
@@ -364,82 +374,84 @@
     lax.fori_loop(0, UB, base_block, 0)
 
     def a_wait(i, carry):
-        a_arrival(K - 1 - i).wait_recv()
+        a_arrival(far_first(i)).wait_recv()
         return carry
 
     lax.fori_loop(0, K - 1, a_wait, 0)
     made = jnp.dot(l_tab[...], part_in[...].reshape(K * ROWS, X), preferred_element_type=F32)
-    asm[core * 4 + z] = jnp.concatenate([made[:S], made[S:]], axis=1).astype(BF16)
-
-    def c_copy(slot, send, there):
+    asm[0, core] = jnp.concatenate([made[:S], made[S:]], axis=1).astype(BF16)
+
+    def c_copy(src, dst, half, send, there):
         return pltpu.make_async_remote_copy(
-            src_ref=asm.at[slot],
-            dst_ref=asm.at[slot],
+            src_ref=asm.at[src, half],
+            dst_ref=asm.at[dst, half],
             send_sem=c_send.at[send],
-            recv_sem=c_recv.at[slot],
+            recv_sem=c_recv.at[dst, half],
             device_id=(me, there),
             device_id_type=MESH,
         )
 
+    def chip(step):
+        return 2 * ((z + step) & 3)
+
     c_copies = [
-        c_copy(core * 4 + z, dz, 2 * ((z + dz) & 3) + core) for dz in (2, 1, 3)
-    ] + [c_copy(core * 4 + z, 0, 2 * z + sibling)]
+        c_copy(0, 3, core, 3, chip(2) + core),
+        c_copy(0, 0, core, 0, chip(0) + sibling),
+        c_copy(0, 2, core, 2, chip(1) + core),
+        c_copy(0, 1, core, 1, chip(3) + core),
+    ]
     for copy in c_copies:
         copy.start()
-    for dz in (1, 3, 2):
-        slot = core * 4 + ((z - dz) & 3)
-        c_copy(slot, dz, 2 * ((z - dz) & 3) + core).wait_recv()
-        forward = c_copy(slot, 3 + dz, 2 * z + sibling)
-        forward.start()
-        c_copies.append(forward)
-    for other in range(4):
-        c_copy(sibling * 4 + other, 0, 2 * z + sibling).wait_recv()
-
-    row = iota((2 * S, 2 * S), 0)
-    lane = iota((2 * S, 2 * S), 1)
-    weave = ((row >> 1) == (lane & (S - 1))) & ((row & 1) == (lane >> 6))
-    weave = jnp.where(weave, 1.0, 0.0).astype(BF16)
-
-    def rest_store(b):
-        lanes = pl.ds(pl.multiple_of(b * X, X), X)
-        return pltpu.make_async_copy(rest_out.at[b], residual.at[:, :, lanes], rest_sem.at[b])
-
-    def grid_block(b, carry):
-        made = jnp.dot(asm[...].reshape(C * S, 2 * X), w_tab[b], preferred_element_type=F32)
-        real = jnp.zeros((S, X), F32)
-        imag = jnp.zeros((S, X), F32)
-        for c in range(C):
-            dr = d_tab[c // 4, b, c % 4 : c % 4 + 1, :X]
-            di = d_tab[c // 4, b, c % 4 : c % 4 + 1, X:]
-            pr = made[c * S : (c + 1) * S, :X]
-            pi = made[c * S : (c + 1) * S, X:]
-            real = real + (pr * dr - pi * di)
-            imag = imag + (pr * di + pi * dr)
-        real = base[b, :, :X] - weight[...] * real
-        imag = base[b, :, X:] - weight[...] * imag
-        rest[b, :, :X] = real
-        rest[b, :, X:] = imag
-        woven = jnp.dot(
-            weave,
-            jnp.concatenate([real, imag], axis=0).astype(BF16),
-            preferred_element_type=F32,
-        )
-        rest_out.at[b].reshape(2 * S, X)[...] = woven.astype(BF16)
-        rest_store(b).start()
-        return carry
-
-    lax.fori_loop(0, UB, grid_block, 0)
-
-    def share_of(parity):
-        share_acc[...] = jnp.zeros_like(share_acc)
+
+    def hand_on(at):
+        c_copy(at, at, core, at, chip(0) + core).wait_recv()
+        copy = c_copy(at, at, core, 3 + at, chip(0) + sibling)
+        copy.start()
+        c_copies.append(copy)
+
+    def grid_part(low, count):
+        def grid_block(b, carry):
+            made = jnp.dot(
+                asm[low : low + count].reshape(count * 2 * S, 2 * X),
+                w_tab[b],
+                preferred_element_type=F32,
+            )
+            real = jnp.zeros((S, X), F32)
+            imag = jnp.zeros((S, X), F32)
+            for c in range(2 * count):
+                dr = d_tab[b, 2 * low + c : 2 * low + c + 1, :X]
+                di = d_tab[b, 2 * low + c : 2 * low + c + 1, X:]
+                pr = made[c * S : (c + 1) * S, :X]
+                pi = made[c * S : (c + 1) * S, X:]
+                real = real + (pr * dr - pi * di)
+                imag = imag + (pr * di + pi * dr)
+            base[b, :, :X] -= weight[...] * real
+            base[b, :, X:] -= weight[...] * imag
+            return carry
+
+        lax.fori_loop(0, UB, grid_block, 0)
+
+    c_copy(0, 0, sibling, 0, chip(0) + sibling).wait_recv()
+    grid_part(0, 1)
+    hand_on(1)
+    hand_on(2)
+    c_copy(1, 1, sibling, 1, chip(0) + sibling).wait_recv()
+    c_copy(2, 2, sibling, 2, chip(0) + sibling).wait_recv()
+    grid_part(1, 2)
+    hand_on(3)
+    c_copy(3, 3, sibling, 3, chip(0) + sibling).wait_recv()
+    grid_part(3, 1)
+
+    def share_part(low, count):
+        share_acc[low : low + count] = jnp.zeros((count, 2, S, 2 * X), F32)
 
         def share_block(b, carry):
-            real = rest[b, :, :X]
-            imag = rest[b, :, X:]
+            real = base[b, :, :X]
+            imag = base[b, :, X:]
             turned = []
-            for c in range(4):
-                dr = d_tab[parity, b, c : c + 1, :X]
-                di = d_tab[parity, b, c : c + 1, X:]
+            for c in range(2 * low, 2 * (low + count)):
+                dr = d_tab[b, c : c + 1, :X]
+                di = d_tab[b, c : c + 1, X:]
                 turned.append(
                     jnp.concatenate(
                         [
@@ -449,57 +461,93 @@
                         axis=1,
                     )
                 )
-            share_acc[...] += lax.dot_general(
+            made = lax.dot_general(
                 jnp.concatenate(turned, axis=0),
                 w_tab[b],
                 (((1,), (1,)), ((), ())),
                 preferred_element_type=F32,
             )
+            share_acc[low : low + count] += made.reshape(count, 2, S, 2 * X)
             return carry
 
         lax.fori_loop(0, UB, share_block, 0)
 
-    share_of(sibling)
-    pair_out[...] = share_acc[...].astype(BF16).reshape(4, S, 2 * X)
-    pair = pltpu.make_async_remote_copy(
-        src_ref=pair_out,
-        dst_ref=pair_in,
-        send_sem=pair_send,
-        recv_sem=pair_recv,
-        device_id=(me, 2 * z + sibling),
-        device_id_type=MESH,
-    )
-    pair.start()
-    share_of(core)
-    pair.wait_recv()
+    def pair_copy(at):
+        return pltpu.make_async_remote_copy(
+            src_ref=pair_out.at[at],
+            dst_ref=pair_in.at[at],
+            send_sem=pair_send.at[at],
+            recv_sem=pair_recv.at[at],
+            device_id=(me, 2 * z + sibling),
+            device_id_type=MESH,
+        )
+
+    def pair_start(at):
+        pair_out[at] = share_acc[at, sibling].astype(BF16)
+        pair_copy(at).start()
 
     def strip_total(at):
-        rows = pl.ds(pl.multiple_of(at * S, S), S)
-        return share_acc[rows, :] + pair_in[at].astype(F32)
-
-    def e_copy(there, slot, dz):
+        pair_copy(at).wait_recv()
+        return share_acc[at, core] + pair_in[at].astype(F32)
+
+    def e_copy(at):
         return pltpu.make_async_remote_copy(
-            src_ref=share_out.at[there],
-            dst_ref=share_in.at[slot],
-            send_sem=e_send.at[dz],
-            recv_sem=e_recv.at[slot],
-            device_id=(me, 2 * there + core),
+            src_ref=share_out.at[at],
+            dst_ref=share_in.at[PLACES.index((4 - PLACES[at]) % 4)],
+            send_sem=e_send.at[at],
+            recv_sem=e_recv.at[PLACES.index((4 - PLACES[at]) % 4)],
+            device_id=(me, chip(PLACES[at]) + core),
             device_id_type=MESH,
         )
 
-    for dz in (2, 1, 3):
-        there = (z + dz) & 3
-        share_out[there] = strip_total(there).astype(BF16)
-        e_copy(there, z, dz).start()
-    total = strip_total(z)
-    for dz in (1, 3, 2):
-        there = (z - dz) & 3
-        e_copy(there, there, dz).wait_recv()
-        total = total + share_in[there].astype(F32)
+    def e_arrival(at):
+        return pltpu.make_async_remote_copy(
+            src_ref=share_out.at[at],
+            dst_ref=share_in.at[at],
+            send_sem=e_send.at[at],
+            recv_sem=e_recv.at[at],
+            device_id=(me, chip(PLACES[at]) + core),
+            device_id_type=MESH,
+        )
+
+    def e_start(at):
+        share_out[at] = strip_total(at).astype(BF16)
+        e_copy(at).start()
+
+    share_part(3, 1)
+    pair_start(3)
+    share_part(0, 3)
+    e_start(3)
+    for at in (1, 2, 0):
+        pair_start(at)
+    e_start(1)
+    e_start(2)
+    total = strip_total(0)
+
+    row = iota((2 * S, 2 * S), 0)
+    lane = iota((2 * S, 2 * S), 1)
+    weave = ((row >> 1) == (lane & (S - 1))) & ((row & 1) == (lane >> 6))
+    weave = jnp.where(weave, 1.0, 0.0).astype(BF16)
+
+    def rest_store(b):
+        lanes = pl.ds(pl.multiple_of(b * X, X), X)
+        return pltpu.make_async_copy(rest_out.at[b], residual.at[:, :, lanes], rest_sem.at[b])
+
+    def rest_block(b, carry):
+        woven = jnp.dot(
+            weave,
+            jnp.concatenate([base[b, :, :X], base[b, :, X:]], axis=0).astype(BF16),
+            preferred_element_type=F32,
+        )
+        rest_out.at[b].reshape(2 * S, X)[...] = woven.astype(BF16)
+        rest_store(b).start()
+        return carry
+
+    lax.fori_loop(0, UB, rest_block, 0)
+    for at in (1, 2, 3):
+        e_arrival(at).wait_recv()
+        total = total + share_in[at].astype(F32)
     share = jnp.concatenate([total[:, :X], total[:, X:]], axis=0).astype(BF16)
-
-    made = jnp.dot(lt_tab[...].reshape(K * ROWS, X), share, preferred_element_type=F32)
-    back_out[...] = made.astype(BF16).reshape(K, ROWS, X)
 
     def f_copy(p):
         there = facet_step(me, p)
@@ -523,23 +571,30 @@
             device_id_type=MESH,
         )
 
-    def f_start(i, carry):
-        f_copy(K - 1 - i).start()
-        return carry
-
-    lax.fori_loop(0, K - 1, f_start, 0)
+    def back_group(a, carry):
+        facet = ((me >> 3) + (far_first(a * 8) >> 3)) & 3
+        made = jnp.dot(lt_tab[facet], share, preferred_element_type=F32)
+        back_out[pl.ds(facet * 8, 8)] = made.astype(BF16).reshape(8, ROWS, X)
+
+        def f_start(i, inner):
+            f_copy(far_first(a * 8 + i)).start()
+            return inner
+
+        lax.fori_loop(0, jnp.where(a == 3, 7, 8), f_start, 0)
+        return carry
+
+    lax.fori_loop(0, 4, back_group, 0)
     back[me] = back_out[me]
     back_acc[...] = jnp.zeros_like(back_acc)
 
     def image_group(i, carry):
-        dx = 3 - i
-        start = (((me >> 3) - dx) & 3) * 8
+        start = (((me >> 3) - (far_first(i * 8) >> 3)) & 3) * 8
 
         def f_wait(j, inner):
-            f_arrival(dx * 8 + j).wait_recv()
+            f_arrival(far_first(i * 8 + j)).wait_recv()
             return inner
 
-        lax.fori_loop(jnp.where(dx == 0, 1, 0), 8, f_wait, 0)
+        lax.fori_loop(0, jnp.where(i == 3, 7, 8), f_wait, 0)
         back_acc[...] += lax.dot_general(
             back[pl.ds(start, 8)].reshape(8 * ROWS, X),
             n_tab[pl.ds(start, 8)].reshape(8 * ROWS, 2 * Y),
@@ -559,9 +614,10 @@
     lax.fori_loop(1, K, sent, 0)
     for copy in c_copies:
         copy.wait_send()
-    pair.wait_send()
-    for dz in (2, 1, 3):
-        e_copy((z + dz) & 3, z, dz).wait_send()
+    for at in range(4):
+        pair_copy(at).wait_send()
+    for at in (1, 2, 3):
+        e_copy(at).wait_send()
 
     def stored(b, carry):
         rest_store(b).wait()
@@ -592,15 +648,15 @@
             jax.ShapeDtypeStruct((S, 2, U), BF16),
             jax.ShapeDtypeStruct((2 * Y, X), BF16),
         ),
-        in_specs=[anywhere] * 11,
+        in_specs=[pl.BlockSpec(memory_space=pltpu.HBM)] * 11,
         out_specs=(anywhere, vmem),
         scratch_shapes=[
             pltpu.SMEM((4,), jnp.int32),
             pltpu.SMEM((C,), jnp.int32),
             pltpu.SMEM((K,), jnp.int32),
             pltpu.SMEM((C,), jnp.int32),
-            pltpu.SMEM((BLOCKS, 1), jnp.int32),
-            pltpu.SMEM((BLOCKS, 8), F32),
+            pltpu.SMEM((1, BLOCKS), jnp.int32),
+            pltpu.SMEM((8, BLOCKS), F32),
             pltpu.VMEM((2 * Y, X), BF16),
             pltpu.VMEM((TERMS, 2 * Y), F32),
             pltpu.VMEM((S, PIECE_COLS), F32),
@@ -612,14 +668,13 @@
             pltpu.VMEM((K, ROWS, X), BF16),
             pltpu.VMEM((2 * S, K * ROWS), BF16),
             pltpu.VMEM((4, PIECE_COLS, 2 * S), BF16),
-            pltpu.VMEM((C, S, 2 * X), BF16),
+            pltpu.VMEM((4, 2, S, 2 * X), BF16),
             pltpu.VMEM((UB, 2 * X, 2 * X), BF16),
-            pltpu.VMEM((2, UB, 4, 2 * X), F32),
+            pltpu.VMEM((UB, C, 2 * X), F32),
             pltpu.VMEM((UB, S, 2 * X), F32),
             pltpu.VMEM((S, X), F32),
-            pltpu.VMEM((UB, S, 2 * X), F32),
             pltpu.VMEM((UB, S, 2, X), BF16),
-            pltpu.VMEM((4 * S, 2 * X), F32),
+            pltpu.VMEM((4, 2, S, 2 * X), F32),
             pltpu.VMEM((4, S, 2 * X), BF16),
             pltpu.VMEM((4, S, 2 * X), BF16),
             pltpu.VMEM((4, S, 2 * X), BF16),
@@ -632,17 +687,17 @@
             dma((UB,)),
             dma((K,)),
             dma((K,)),
-            dma((8,)),
-            dma((C,)),
-            dma,
-            dma,
+            dma((7,)),
+            dma((4, 2)),
+            dma((4,)),
+            dma((4,)),
             dma((4,)),
             dma((4,)),
             dma((K,)),
             dma((K,)),
         ],
         compiler_params=pltpu.CompilerParams(
-            collective_id=0, has_side_effects=True, vmem_limit_bytes=48 * 1024 * 1024
+            collective_id=0, has_side_effects=True, vmem_limit_bytes=60 * 1024 * 1024
         ),
     )(
         facet_off,
@@ -652,8 +707,8 @@
         facet_strips.reshape(2 * Y, X),
         jnp.asarray(b),
         jnp.asarray(q),
-        block_band,
-        vis_weight,
+        block_band.T,
+        vis_weight.T,
         screen_phase,
         visibilities.reshape(BLOCKS * 8, 2, U),
     )

time: 58.1 us -> 52.4 us (0.902)
  local copies, waits for them, and re-layouts: 8.16 us -> 2.58 us
    unnamed x26 -> x4, local copies, waits for them, and re-layouts: 8.16 us -> 2.58 us
where the time goes in v2:
time: 52.4 us; the launch traced here: 52.2 us
  Pallas kernels  49 us (94%)
  local copies, waits for them, and re-layouts  2.58 us (5%)
  between operations  0.65 us (1%)
    pallas_call x1, Pallas kernels, shards(): pl.pallas_call(kernel, name='imaging_round', out_shape=(jax.ShapeDtypeStr...  49 us
    unnamed x4, local copies, waits for them, and re-layouts  2.58 us

profile of v2, /device:TPU:1, one launch (start us, length us, event | category | flops | bytes accessed | tf_op | source)
XLA Modules:
  0.0 52.2 jit_solution(6529297134352140191)
XLA Ops:
  0.6 49.0 %imaging_round.1 = (bf16[64,2,1024]{2,1,0:T(2,128)(2,1)}, bf16[1024,128]{1,0:T(8,128)(2,1)}) custom-call(s32[4]{0:T(128)} %facet_off_hbm.1, s32[8]{0:T(128)} %strip_off_hbm.1, s32[32]{0:T(128)} %sub_v_hbm.1, s32[8]{0:T(128)} %sub_u_hbm.1, bf16[1024,128]{1,0:T(8,128)(2,1)} %bitcast.7, f32[24,1024]{1,0:T(8,128)} %constant.4.clone.b_hbm, ...), custom_call_target="tpu_custom_call" | custom-call | tf_op jit(solution)/shard_map/imaging_round/pallas_call | solution.py:644
  49.6 0.0 copy-start
  49.7 1.9 %copy.15 = bf16[64,2,1024]{2,1,0:T(2,128)(2,1)} copy(bf16[64,2,1024]{2,1,0:T(2,128)(2,1)} %get-tuple-element.8) | data formatting | bytes 524288
  51.5 0.0 copy-done
  51.5 0.7 %copy.16 = bf16[512,2,128]{2,1,0:T(2,128)(2,1)} copy(bf16[512,2,128]{2,1,0:T(2,128)(2,1)S(1)} %bitcast.6) | data formatting | bytes 524288
Async XLA Ops:
  49.6 1.9 %copy-start = (bf16[1024,128]{1,0:T(8,128)(2,1)S(1)}, bf16[1024,128]{1,0:T(8,128)(2,1)}, u32[]{:S(2)}) copy-start(bf16[1024,128]{1,0:T(8,128)(2,1)} %get-tuple-element.5) | copy-start | bytes 786436

commit v3 on v2

--- a/solution.py
+++ b/solution.py
@@ -24,9 +24,10 @@
 UB = U // X
 BLOCKS = 16
 PLACES = (0, 1, 3, 2)
-HALF = 12
+HALF = 10
 TERMS = 2 * HALF
-ROWS = 2 * TERMS
+SENT = 2 * TERMS
+ROWS = 48
 PIECE_COLS = PIECES * ROWS
 
 
@@ -42,10 +43,9 @@
         right.append(v[:HALF])
     q = np.concatenate(left, axis=1) / 1024.0
     b = np.concatenate(right, axis=0)
-    return (
-        np.tile(q, (1, 2 * PIECES)).astype(np.float32),
-        np.repeat(b, 2, axis=1).astype(np.float32),
-    )
+    q = np.pad(np.tile(q, (1, 2)), ((0, 0), (0, ROWS - SENT)))
+    b = np.tile(np.repeat(b, 2, axis=1), (2, 1))
+    return np.tile(q, (1, PIECES)).astype(np.float32), b.astype(np.float32)
 
 
 def quarter_turns(q, t):
@@ -183,6 +183,9 @@
     ]
     for load in loads[:4]:
         load.start()
+    pad = slice(32, ROWS)
+    part_in[:, pad] = jnp.zeros((K, ROWS - 32, X), BF16)
+    back[:, pad] = jnp.zeros((K, ROWS - 32, X), BF16)
     barrier = pltpu.get_barrier_semaphore()
 
     def greet_facet(i, carry):
@@ -192,8 +195,14 @@
         return carry
 
     lax.fori_loop(0, K - 1, greet_facet, 0)
-    for other in [2 * z + sibling] + [2 * ((z + dz) & 3) + core for dz in (1, 2, 3)]:
-        pl.semaphore_signal(barrier, inc=1, device_id=(me, other), device_id_type=MESH)
+    for step in (2, 1, 3, 0):
+        for half in (0, 1)[step == 0 :]:
+            pl.semaphore_signal(
+                barrier,
+                inc=1,
+                device_id=(me, 2 * ((z + step) & 3) + (core ^ half)),
+                device_id_type=MESH,
+            )
     for load in loads[4:]:
         load.start()
 
@@ -227,15 +236,17 @@
 
     lax.fori_loop(0, K // 8, mod_rows, 0)
 
+    is_real = iota((SENT, X), 0) < TERMS
+    padding = jnp.zeros((ROWS - SENT, X), F32)
+
     def facet_group(g, carry):
         for h in range(2 * Y // X):
             lanes = slice(h * X, (h + 1) * X)
             upper = slice(2 * Y + h * X, 2 * Y + (h + 1) * X)
             b = b_tab[:, lanes]
             for i in range(4):
-                n_tab[g * 4 + i, :, lanes] = jnp.concatenate(
-                    [b * mod[g, i : i + 1, lanes], b * mod[g, i : i + 1, upper]], axis=0
-                ).astype(BF16)
+                turn = jnp.where(is_real, mod[g, i : i + 1, lanes], mod[g, i : i + 1, upper])
+                n_tab[g * 4 + i, :, lanes] = jnp.concatenate([b * turn, padding], axis=0).astype(BF16)
         made = jnp.dot(
             n_tab[pl.ds(g * 4, 4)].reshape(4 * ROWS, 2 * Y),
             strips[...],
@@ -244,14 +255,14 @@
         part_out[pl.ds(g * 4, 4)] = made.astype(BF16).reshape(4, ROWS, X)
         return carry
 
-    lax.fori_loop(0, K // 4, facet_group, 0)
-    pl.semaphore_wait(barrier, K - 1 + 4)
+    lax.fori_loop(0, K // 4, facet_group, 0, unroll=2)
+    pl.semaphore_wait(barrier, K - 1 + C - 1)
 
     def a_copy(p):
         there = facet_step(me, p)
         return pltpu.make_async_remote_copy(
-            src_ref=part_out.at[there],
-            dst_ref=part_in.at[me],
+            src_ref=part_out.at[there, :SENT],
+            dst_ref=part_in.at[me, :SENT],
             send_sem=a_send.at[p],
             recv_sem=a_recv.at[me],
             device_id=(there, col),
@@ -261,8 +272,8 @@
     def a_arrival(p):
         source = facet_step(me, back_step(p))
         return pltpu.make_async_remote_copy(
-            src_ref=part_out.at[source],
-            dst_ref=part_in.at[source],
+            src_ref=part_out.at[source, :SENT],
+            dst_ref=part_in.at[source, :SENT],
             send_sem=a_send.at[p],
             recv_sem=a_recv.at[source],
             device_id=(source, col),
@@ -276,7 +287,7 @@
     lax.fori_loop(0, K - 1, a_start, 0)
     part_in[me] = part_out[me]
 
-    for load in loads[4:]:
+    for load in loads[8:]:
         load.wait()
 
     l_lane = iota((8, PIECE_COLS), 1)
@@ -302,10 +313,44 @@
         )
         made = jnp.dot(left, right, precision=lax.Precision.HIGHEST, preferred_element_type=F32)
         l_tab[:, pl.ds(pl.multiple_of(f * PIECE_COLS, X), PIECE_COLS)] = made.astype(BF16)
-        lt_tab[f] = made.T.astype(BF16)
         return carry
 
     lax.fori_loop(0, 4, l_facet, 0)
+    def a_wait(i, carry):
+        a_arrival(far_first(i)).wait_recv()
+        return carry
+
+    lax.fori_loop(0, K - 1, a_wait, 0)
+    made = jnp.dot(l_tab[...], part_in[...].reshape(K * ROWS, X), preferred_element_type=F32)
+    asm[0, 0] = jnp.concatenate([made[:S], made[S:]], axis=1).astype(BF16)
+
+    def c_copy(src, dst, half, send, there):
+        return pltpu.make_async_remote_copy(
+            src_ref=asm.at[src, 0],
+            dst_ref=asm.at[dst, half],
+            send_sem=c_send.at[send],
+            recv_sem=c_recv.at[dst, half],
+            device_id=(me, there),
+            device_id_type=MESH,
+        )
+
+    def chip(step):
+        return 2 * ((z + step) & 3)
+
+    c_copies = [
+        c_copy(0, 3, 0, 6, chip(2) + core),
+        c_copy(0, 3, 1, 7, chip(2) + sibling),
+        c_copy(0, 0, 1, 0, chip(0) + sibling),
+        c_copy(0, 2, 0, 2, chip(1) + core),
+        c_copy(0, 1, 0, 3, chip(3) + core),
+        c_copy(0, 2, 1, 4, chip(1) + sibling),
+        c_copy(0, 1, 1, 5, chip(3) + sibling),
+    ]
+    for copy in c_copies:
+        copy.start()
+
+    for load in loads[4:8]:
+        load.wait()
     frequency = sub_u[col]
 
     def w_block(b, carry):
@@ -327,7 +372,7 @@
     for at, step in enumerate(PLACES):
         for c in range(2):
             strip = jnp.where(
-                iota((C, X), 0) == 2 * at + c, strip_off[2 * ((z + step) & 3) + c], strip
+                iota((C, X), 0) == 2 * at + c, strip_off[2 * ((z + step) & 3) + (core ^ c)], strip
             )
 
     def d_block(b, carry):
@@ -373,41 +418,8 @@
 
     lax.fori_loop(0, UB, base_block, 0)
 
-    def a_wait(i, carry):
-        a_arrival(far_first(i)).wait_recv()
-        return carry
-
-    lax.fori_loop(0, K - 1, a_wait, 0)
-    made = jnp.dot(l_tab[...], part_in[...].reshape(K * ROWS, X), preferred_element_type=F32)
-    asm[0, core] = jnp.concatenate([made[:S], made[S:]], axis=1).astype(BF16)
-
-    def c_copy(src, dst, half, send, there):
-        return pltpu.make_async_remote_copy(
-            src_ref=asm.at[src, half],
-            dst_ref=asm.at[dst, half],
-            send_sem=c_send.at[send],
-            recv_sem=c_recv.at[dst, half],
-            device_id=(me, there),
-            device_id_type=MESH,
-        )
-
-    def chip(step):
-        return 2 * ((z + step) & 3)
-
-    c_copies = [
-        c_copy(0, 3, core, 3, chip(2) + core),
-        c_copy(0, 0, core, 0, chip(0) + sibling),
-        c_copy(0, 2, core, 2, chip(1) + core),
-        c_copy(0, 1, core, 1, chip(3) + core),
-    ]
-    for copy in c_copies:
-        copy.start()
-
-    def hand_on(at):
-        c_copy(at, at, core, at, chip(0) + core).wait_recv()
-        copy = c_copy(at, at, core, 3 + at, chip(0) + sibling)
-        copy.start()
-        c_copies.append(copy)
+    def c_wait(at, half):
+        c_copy(at, at, half, 0, chip(0) + sibling).wait_recv()
 
     def grid_part(low, count):
         def grid_block(b, carry):
@@ -429,27 +441,23 @@
             base[b, :, X:] -= weight[...] * imag
             return carry
 
-        lax.fori_loop(0, UB, grid_block, 0)
-
-    c_copy(0, 0, sibling, 0, chip(0) + sibling).wait_recv()
-    grid_part(0, 1)
-    hand_on(1)
-    hand_on(2)
-    c_copy(1, 1, sibling, 1, chip(0) + sibling).wait_recv()
-    c_copy(2, 2, sibling, 2, chip(0) + sibling).wait_recv()
-    grid_part(1, 2)
-    hand_on(3)
-    c_copy(3, 3, sibling, 3, chip(0) + sibling).wait_recv()
-    grid_part(3, 1)
-
-    def share_part(low, count):
-        share_acc[low : low + count] = jnp.zeros((count, 2, S, 2 * X), F32)
+        lax.fori_loop(0, UB, grid_block, 0, unroll=4)
+
+    for at in range(4):
+        if at:
+            c_wait(at, 0)
+        c_wait(at, 1)
+    grid_part(0, 4)
+
+    def share_part(low, high):
+        rows = slice(low * S, high * S)
+        share_acc[rows, :] = jnp.zeros(((high - low) * S, 2 * X), F32)
 
         def share_block(b, carry):
             real = base[b, :, :X]
             imag = base[b, :, X:]
             turned = []
-            for c in range(2 * low, 2 * (low + count)):
+            for c in range(low, high):
                 dr = d_tab[b, c : c + 1, :X]
                 di = d_tab[b, c : c + 1, X:]
                 turned.append(
@@ -461,16 +469,15 @@
                         axis=1,
                     )
                 )
-            made = lax.dot_general(
+            share_acc[rows, :] += lax.dot_general(
                 jnp.concatenate(turned, axis=0),
                 w_tab[b],
                 (((1,), (1,)), ((), ())),
                 preferred_element_type=F32,
             )
-            share_acc[low : low + count] += made.reshape(count, 2, S, 2 * X)
             return carry
 
-        lax.fori_loop(0, UB, share_block, 0)
+        lax.fori_loop(0, UB, share_block, 0, unroll=4)
 
     def pair_copy(at):
         return pltpu.make_async_remote_copy(
@@ -483,12 +490,12 @@
         )
 
     def pair_start(at):
-        pair_out[at] = share_acc[at, sibling].astype(BF16)
+        pair_out[at] = share_acc[(2 * at + 1) * S : (2 * at + 2) * S, :].astype(BF16)
         pair_copy(at).start()
 
     def strip_total(at):
         pair_copy(at).wait_recv()
-        return share_acc[at, core] + pair_in[at].astype(F32)
+        return share_acc[2 * at * S : (2 * at + 1) * S, :] + pair_in[at].astype(F32)
 
     def e_copy(at):
         return pltpu.make_async_remote_copy(
@@ -514,12 +521,14 @@
         share_out[at] = strip_total(at).astype(BF16)
         e_copy(at).start()
 
-    share_part(3, 1)
+    share_part(7, 8)
     pair_start(3)
-    share_part(0, 3)
+    share_part(2, 7)
+    pair_start(1)
+    pair_start(2)
     e_start(3)
-    for at in (1, 2, 0):
-        pair_start(at)
+    share_part(0, 2)
+    pair_start(0)
     e_start(1)
     e_start(2)
     total = strip_total(0)
@@ -543,7 +552,13 @@
         rest_store(b).start()
         return carry
 
-    lax.fori_loop(0, UB, rest_block, 0)
+    lax.fori_loop(0, UB, rest_block, 0, unroll=4)
+
+    def turn_table(f, carry):
+        lt_tab[f] = l_tab[:, pl.ds(pl.multiple_of(f * PIECE_COLS, X), PIECE_COLS)].T
+        return carry
+
+    lax.fori_loop(0, 4, turn_table, 0)
     for at in (1, 2, 3):
         e_arrival(at).wait_recv()
         total = total + share_in[at].astype(F32)
@@ -552,8 +567,8 @@
     def f_copy(p):
         there = facet_step(me, p)
         return pltpu.make_async_remote_copy(
-            src_ref=back_out.at[there],
-            dst_ref=back.at[me],
+            src_ref=back_out.at[there, :SENT],
+            dst_ref=back.at[me, :SENT],
             send_sem=f_send.at[p],
             recv_sem=f_recv.at[me],
             device_id=(there, col),
@@ -563,8 +578,8 @@
     def f_arrival(p):
         source = facet_step(me, back_step(p))
         return pltpu.make_async_remote_copy(
-            src_ref=back_out.at[source],
-            dst_ref=back.at[source],
+            src_ref=back_out.at[source, :SENT],
+            dst_ref=back.at[source, :SENT],
             send_sem=f_send.at[p],
             recv_sem=f_recv.at[source],
             device_id=(source, col),
@@ -624,6 +639,17 @@
         return carry
 
     lax.fori_loop(0, UB, stored, 0)
+
+
+def store(residual, image, residual_out, image_out, sem):
+    copies = [
+        pltpu.make_async_copy(residual, residual_out, sem.at[0]),
+        pltpu.make_async_copy(image, image_out, sem.at[1]),
+    ]
+    for copy in copies:
+        copy.start()
+    for copy in copies:
+        copy.wait()
 
 
 def shards(
@@ -658,7 +684,7 @@
             pltpu.SMEM((1, BLOCKS), jnp.int32),
             pltpu.SMEM((8, BLOCKS), F32),
             pltpu.VMEM((2 * Y, X), BF16),
-            pltpu.VMEM((TERMS, 2 * Y), F32),
+            pltpu.VMEM((SENT, 2 * Y), F32),
             pltpu.VMEM((S, PIECE_COLS), F32),
             pltpu.VMEM((S, U), F32),
             pltpu.VMEM((UB, BLOCKS * 8, 2, X), BF16),
@@ -674,7 +700,7 @@
             pltpu.VMEM((UB, S, 2 * X), F32),
             pltpu.VMEM((S, X), F32),
             pltpu.VMEM((UB, S, 2, X), BF16),
-            pltpu.VMEM((4, 2, S, 2 * X), F32),
+            pltpu.VMEM((C * S, 2 * X), F32),
             pltpu.VMEM((4, S, 2 * X), BF16),
             pltpu.VMEM((4, S, 2 * X), BF16),
             pltpu.VMEM((4, S, 2 * X), BF16),
@@ -687,7 +713,7 @@
             dma((UB,)),
             dma((K,)),
             dma((K,)),
-            dma((7,)),
+            dma((8,)),
             dma((4, 2)),
             dma((4,)),
             dma((4,)),
@@ -697,20 +723,40 @@
             dma((K,)),
         ],
         compiler_params=pltpu.CompilerParams(
-            collective_id=0, has_side_effects=True, vmem_limit_bytes=60 * 1024 * 1024
+            collective_id=0, has_side_effects=True, vmem_limit_bytes=48 * 1024 * 1024
         ),
     )(
-        facet_off,
-        strip_off,
-        sub_v,
-        sub_u,
-        facet_strips.reshape(2 * Y, X),
-        jnp.asarray(b),
-        jnp.asarray(q),
-        block_band.T,
-        vis_weight.T,
-        screen_phase,
-        visibilities.reshape(BLOCKS * 8, 2, U),
+        *(
+            pltpu.with_memory_space_constraint(array, pltpu.HBM)
+            for array in (
+                facet_off,
+                strip_off,
+                sub_v,
+                sub_u,
+                facet_strips.reshape(2 * Y, X),
+                jnp.asarray(b),
+                jnp.asarray(q),
+                block_band.T,
+                vis_weight.T,
+                screen_phase,
+                visibilities.reshape(BLOCKS * 8, 2, U),
+            )
+        )
+    )
+    hbm = pl.BlockSpec(memory_space=pltpu.HBM)
+    residual, image = pl.pallas_call(
+        store,
+        name="store",
+        out_shape=(
+            jax.ShapeDtypeStruct((S, 2, U), BF16),
+            jax.ShapeDtypeStruct((2 * Y, X), BF16),
+        ),
+        in_specs=[anywhere, anywhere],
+        out_specs=(hbm, hbm),
+        scratch_shapes=[dma((2,))],
+    )(
+        pltpu.with_memory_space_constraint(residual, pltpu.VMEM),
+        pltpu.with_memory_space_constraint(image, pltpu.VMEM),
     )
     return residual, image.reshape(Y, 2, X)
 

time: 52.4 us -> 44.8 us (0.85)
  Pallas kernels: 49 us -> 44.1 us
  local copies, waits for them, and re-layouts: 2.58 us -> 0 us
    pallas_call x1, Pallas kernels: 49 us -> 43.3 us  [shards(): pl.pallas_call(kernel, name='imaging_round', out_shape=(jax.ShapeDtypeStr...]
    unnamed x4 -> x0, local copies, waits for them, and re-layouts: 2.58 us -> none
    pallas_call x0 -> x1, Pallas kernels: none -> 0.81 us  [shards(): pl.pallas_call(store, name='store', out_shape=(jax.ShapeDtypeStruct((S, 2...]
where the time goes in v3:
time: 44.8 us; the launch traced here: 44.7 us
  Pallas kernels  44.1 us (98%)
  between operations  0.64 us (1%)
    pallas_call x1, Pallas kernels, shards(): pl.pallas_call(kernel, name='imaging_round', out_shape=(jax.ShapeDtypeStr...  43.3 us

profile of v3, /device:TPU:1, one launch (start us, length us, event | category | flops | bytes accessed | tf_op | source)
XLA Modules:
  0.0 44.7 jit_solution(10766570917348182408)
XLA Ops:
  0.6 43.3 %imaging_round.1 = (bf16[64,2,1024]{2,1,0:T(2,128)(2,1)S(1)}, bf16[1024,128]{1,0:T(8,128)(2,1)S(1)}) custom-call(s32[4]{0:T(128)} %facet_off_hbm.1, s32[8]{0:T(128)} %strip_off_hbm.1, s32[32]{0:T(128)} %sub_v_hbm.1, s32[8]{0:T(128)} %sub_u_hbm.1, bf16[1024,128]{1,0:T(8,128)(2,1)} %bitcast.6, f32[40,1024]{1,0:T(8,128)} %constant.4.clone.b_hbm, ...), custom_call_target="tpu_custom_call" | custom-call | tf_op jit(solution)/shard_map/imaging_round/pallas_call | solution.py:670
  43.9 0.8 %store.1 = (bf16[64,2,1024]{2,1,0:T(2,128)(2,1)}, bf16[1024,128]{1,0:T(8,128)(2,1)}) custom-call(bf16[64,2,1024]{2,1,0:T(2,128)(2,1)S(1)} %get-tuple-element.6.residual, bf16[1024,128]{1,0:T(8,128)(2,1)S(1)} %get-tuple-element.7.image), custom_call_target="tpu_custom_call" | custom-call | tf_op jit(solution)/shard_map/store/pallas_call | solution.py:747

commit v4 on v3

--- a/solution.py
+++ b/solution.py
@@ -234,7 +234,7 @@
                 mod[i * 2 + g, :, 2 * Y + h * X : 2 * Y + (h + 1) * X] = imag[g * 4 : g * 4 + 4]
         return carry
 
-    lax.fori_loop(0, K // 8, mod_rows, 0)
+    lax.fori_loop(0, K // 8, mod_rows, 0, unroll=2)
 
     is_real = iota((SENT, X), 0) < TERMS
     padding = jnp.zeros((ROWS - SENT, X), F32)
@@ -255,7 +255,7 @@
         part_out[pl.ds(g * 4, 4)] = made.astype(BF16).reshape(4, ROWS, X)
         return carry
 
-    lax.fori_loop(0, K // 4, facet_group, 0, unroll=2)
+    lax.fori_loop(0, K // 4, facet_group, 0, unroll=4)
     pl.semaphore_wait(barrier, K - 1 + C - 1)
 
     def a_copy(p):
@@ -343,8 +343,6 @@
         c_copy(0, 0, 1, 0, chip(0) + sibling),
         c_copy(0, 2, 0, 2, chip(1) + core),
         c_copy(0, 1, 0, 3, chip(3) + core),
-        c_copy(0, 2, 1, 4, chip(1) + sibling),
-        c_copy(0, 1, 1, 5, chip(3) + sibling),
     ]
     for copy in c_copies:
         copy.start()
@@ -443,11 +441,19 @@
 
         lax.fori_loop(0, UB, grid_block, 0, unroll=4)
 
-    for at in range(4):
-        if at:
-            c_wait(at, 0)
-        c_wait(at, 1)
-    grid_part(0, 4)
+    c_wait(0, 1)
+    grid_part(0, 1)
+    for at in (1, 2):
+        c_wait(at, 0)
+        forward = c_copy(at, at, 1, 3 + at, chip(0) + sibling)
+        forward.start()
+        c_copies.append(forward)
+    c_wait(1, 1)
+    c_wait(2, 1)
+    grid_part(1, 2)
+    c_wait(3, 0)
+    c_wait(3, 1)
+    grid_part(3, 1)
 
     def share_part(low, high):
         rows = slice(low * S, high * S)
@@ -595,12 +601,12 @@
             f_copy(far_first(a * 8 + i)).start()
             return inner
 
-        lax.fori_loop(0, jnp.where(a == 3, 7, 8), f_start, 0)
-        return carry
-
-    lax.fori_loop(0, 4, back_group, 0)
+        lax.fori_loop(0, 7 if a == 3 else 8, f_start, 0)
+        return carry
+
+    for a in range(4):
+        back_group(a, 0)
     back[me] = back_out[me]
-    back_acc[...] = jnp.zeros_like(back_acc)
 
     def image_group(i, carry):
         start = (((me >> 3) - (far_first(i * 8) >> 3)) & 3) * 8
@@ -609,16 +615,18 @@
             f_arrival(far_first(i * 8 + j)).wait_recv()
             return inner
 
-        lax.fori_loop(0, jnp.where(i == 3, 7, 8), f_wait, 0)
-        back_acc[...] += lax.dot_general(
+        lax.fori_loop(0, 7 if i == 3 else 8, f_wait, 0)
+        made = lax.dot_general(
             back[pl.ds(start, 8)].reshape(8 * ROWS, X),
             n_tab[pl.ds(start, 8)].reshape(8 * ROWS, 2 * Y),
             (((0,), (0,)), ((), ())),
             preferred_element_type=F32,
         )
-        return carry
-
-    lax.fori_loop(0, 4, image_group, 0)
+        back_acc[...] = made if i == 0 else back_acc[...] + made
+        return carry
+
+    for i in range(4):
+        image_group(i, 0)
     image[...] = (back_acc[...].T * (1.0 / 32.0)).astype(BF16)
 
     def sent(p, carry):

time: 44.8 us -> 43.9 us (0.980)
  Pallas kernels: 44.1 us -> 43 us
    pallas_call x1, Pallas kernels: 43.3 us -> 42.2 us  [shards(): pl.pallas_call(kernel, name='imaging_round', out_shape=(jax.ShapeDtypeStr...]
where the time goes in v4:
time: 43.9 us; the launch traced here: 43.6 us
  Pallas kernels  43 us (98%)
  between operations  0.64 us (1%)
    pallas_call x1, Pallas kernels, shards(): pl.pallas_call(kernel, name='imaging_round', out_shape=(jax.ShapeDtypeStr...  42.2 us

profile of v4, /device:TPU:1, one launch (start us, length us, event | category | flops | bytes accessed | tf_op | source)
XLA Modules:
  0.0 43.6 jit_solution(7684308312328766047)
XLA Ops:
  0.6 42.2 %imaging_round.1 = (bf16[64,2,1024]{2,1,0:T(2,128)(2,1)S(1)}, bf16[1024,128]{1,0:T(8,128)(2,1)S(1)}) custom-call(s32[4]{0:T(128)} %facet_off_hbm.1, s32[8]{0:T(128)} %strip_off_hbm.1, s32[32]{0:T(128)} %sub_v_hbm.1, s32[8]{0:T(128)} %sub_u_hbm.1, bf16[1024,128]{1,0:T(8,128)(2,1)} %bitcast.6, f32[40,1024]{1,0:T(8,128)} %constant.4.clone.b_hbm, ...), custom_call_target="tpu_custom_call" | custom-call | tf_op jit(solution)/shard_map/imaging_round/pallas_call | solution.py:678
  42.8 0.8 %store.1 = (bf16[64,2,1024]{2,1,0:T(2,128)(2,1)}, bf16[1024,128]{1,0:T(8,128)(2,1)}) custom-call(bf16[64,2,1024]{2,1,0:T(2,128)(2,1)S(1)} %get-tuple-element.6.residual, bf16[1024,128]{1,0:T(8,128)(2,1)S(1)} %get-tuple-element.7.image), custom_call_target="tpu_custom_call" | custom-call | tf_op jit(solution)/shard_map/store/pallas_call | solution.py:755

commit v5 on v4

--- a/solution.py
+++ b/solution.py
@@ -416,6 +416,12 @@
 
     lax.fori_loop(0, UB, base_block, 0)
 
+    def turn_table(f, carry):
+        lt_tab[f] = l_tab[:, pl.ds(pl.multiple_of(f * PIECE_COLS, X), PIECE_COLS)].T
+        return carry
+
+    lax.fori_loop(0, 4, turn_table, 0)
+
     def c_wait(at, half):
         c_copy(at, at, half, 0, chip(0) + sibling).wait_recv()
 
@@ -560,11 +566,6 @@
 
     lax.fori_loop(0, UB, rest_block, 0, unroll=4)
 
-    def turn_table(f, carry):
-        lt_tab[f] = l_tab[:, pl.ds(pl.multiple_of(f * PIECE_COLS, X), PIECE_COLS)].T
-        return carry
-
-    lax.fori_loop(0, 4, turn_table, 0)
     for at in (1, 2, 3):
         e_arrival(at).wait_recv()
         total = total + share_in[at].astype(F32)

time: 43.9 us -> 43.9 us (level)
  no operation moved by 1% of the time
where the time goes in v5:
time: 43.9 us; the launch traced here: 43.6 us
  Pallas kernels  43 us (98%)
  between operations  0.64 us (1%)
    pallas_call x1, Pallas kernels, shards(): pl.pallas_call(kernel, name='imaging_round', out_shape=(jax.ShapeDtypeStr...  42.2 us

profile of v5, /device:TPU:1, one launch (start us, length us, event | category | flops | bytes accessed | tf_op | source)
XLA Modules:
  0.0 43.6 jit_solution(546790067471761991)
XLA Ops:
  0.6 42.2 %imaging_round.1 = (bf16[64,2,1024]{2,1,0:T(2,128)(2,1)S(1)}, bf16[1024,128]{1,0:T(8,128)(2,1)S(1)}) custom-call(s32[4]{0:T(128)} %facet_off_hbm.1, s32[8]{0:T(128)} %strip_off_hbm.1, s32[32]{0:T(128)} %sub_v_hbm.1, s32[8]{0:T(128)} %sub_u_hbm.1, bf16[1024,128]{1,0:T(8,128)(2,1)} %bitcast.6, f32[40,1024]{1,0:T(8,128)} %constant.4.clone.b_hbm, ...), custom_call_target="tpu_custom_call" | custom-call | tf_op jit(solution)/shard_map/imaging_round/pallas_call | solution.py:679
  42.8 0.8 %store.1 = (bf16[64,2,1024]{2,1,0:T(2,128)(2,1)}, bf16[1024,128]{1,0:T(8,128)(2,1)}) custom-call(bf16[64,2,1024]{2,1,0:T(2,128)(2,1)S(1)} %get-tuple-element.6.residual, bf16[1024,128]{1,0:T(8,128)(2,1)S(1)} %get-tuple-element.7.image), custom_call_target="tpu_custom_call" | custom-call | tf_op jit(solution)/shard_map/store/pallas_call | solution.py:756

commit v6 on v5

--- a/solution.py
+++ b/solution.py
@@ -489,7 +489,7 @@
             )
             return carry
 
-        lax.fori_loop(0, UB, share_block, 0, unroll=4)
+        lax.fori_loop(0, UB, share_block, 0, unroll=8 if high - low < 3 else 4)
 
     def pair_copy(at):
         return pltpu.make_async_remote_copy(

time: 43.9 us -> 43.7 us (level)
  no operation moved by 1% of the time
where the time goes in v6:
time: 43.7 us; the launch traced here: 43.6 us
  Pallas kernels  43 us (98%)
  between operations  0.64 us (1%)
    pallas_call x1, Pallas kernels, shards(): pl.pallas_call(kernel, name='imaging_round', out_shape=(jax.ShapeDtypeStr...  42.2 us

profile of v6, /device:TPU:1, one launch (start us, length us, event | category | flops | bytes accessed | tf_op | source)
XLA Modules:
  0.0 43.6 jit_solution(5060660251577194806)
XLA Ops:
  0.6 42.2 %imaging_round.1 = (bf16[64,2,1024]{2,1,0:T(2,128)(2,1)S(1)}, bf16[1024,128]{1,0:T(8,128)(2,1)S(1)}) custom-call(s32[4]{0:T(128)} %facet_off_hbm.1, s32[8]{0:T(128)} %strip_off_hbm.1, s32[32]{0:T(128)} %sub_v_hbm.1, s32[8]{0:T(128)} %sub_u_hbm.1, bf16[1024,128]{1,0:T(8,128)(2,1)} %bitcast.6, f32[40,1024]{1,0:T(8,128)} %constant.4.clone.b_hbm, ...), custom_call_target="tpu_custom_call" | custom-call | tf_op jit(solution)/shard_map/imaging_round/pallas_call | solution.py:679
  42.8 0.8 %store.1 = (bf16[64,2,1024]{2,1,0:T(2,128)(2,1)}, bf16[1024,128]{1,0:T(8,128)(2,1)}) custom-call(bf16[64,2,1024]{2,1,0:T(2,128)(2,1)S(1)} %get-tuple-element.6.residual, bf16[1024,128]{1,0:T(8,128)(2,1)S(1)} %get-tuple-element.7.image), custom_call_target="tpu_custom_call" | custom-call | tf_op jit(solution)/shard_map/store/pallas_call | solution.py:756

commit v7 on v6

--- a/solution.py
+++ b/solution.py
@@ -315,7 +315,7 @@
         l_tab[:, pl.ds(pl.multiple_of(f * PIECE_COLS, X), PIECE_COLS)] = made.astype(BF16)
         return carry
 
-    lax.fori_loop(0, 4, l_facet, 0)
+    lax.fori_loop(0, 4, l_facet, 0, unroll=2)
     def a_wait(i, carry):
         a_arrival(far_first(i)).wait_recv()
         return carry
@@ -414,7 +414,7 @@
         base[b, :, X:] = imag * cos - real * sin
         return carry
 
-    lax.fori_loop(0, UB, base_block, 0)
+    lax.fori_loop(0, UB, base_block, 0, unroll=2)
 
     def turn_table(f, carry):
         lt_tab[f] = l_tab[:, pl.ds(pl.multiple_of(f * PIECE_COLS, X), PIECE_COLS)].T

time: 43.7 us -> 43.7 us (level)
  no operation moved by 1% of the time
where the time goes in v7:
time: 43.7 us; the launch traced here: 43.6 us
  Pallas kernels  43 us (98%)
  between operations  0.64 us (1%)
    pallas_call x1, Pallas kernels, shards(): pl.pallas_call(kernel, name='imaging_round', out_shape=(jax.ShapeDtypeStr...  42.2 us

profile of v7, /device:TPU:1, one launch (start us, length us, event | category | flops | bytes accessed | tf_op | source)
XLA Modules:
  0.0 43.6 jit_solution(18417082495151893030)
XLA Ops:
  0.6 42.2 %imaging_round.1 = (bf16[64,2,1024]{2,1,0:T(2,128)(2,1)S(1)}, bf16[1024,128]{1,0:T(8,128)(2,1)S(1)}) custom-call(s32[4]{0:T(128)} %facet_off_hbm.1, s32[8]{0:T(128)} %strip_off_hbm.1, s32[32]{0:T(128)} %sub_v_hbm.1, s32[8]{0:T(128)} %sub_u_hbm.1, bf16[1024,128]{1,0:T(8,128)(2,1)} %bitcast.6, f32[40,1024]{1,0:T(8,128)} %constant.4.clone.b_hbm, ...), custom_call_target="tpu_custom_call" | custom-call | tf_op jit(solution)/shard_map/imaging_round/pallas_call | solution.py:679
  42.8 0.8 %store.1 = (bf16[64,2,1024]{2,1,0:T(2,128)(2,1)}, bf16[1024,128]{1,0:T(8,128)(2,1)}) custom-call(bf16[64,2,1024]{2,1,0:T(2,128)(2,1)S(1)} %get-tuple-element.6.residual, bf16[1024,128]{1,0:T(8,128)(2,1)S(1)} %get-tuple-element.7.image), custom_call_target="tpu_custom_call" | custom-call | tf_op jit(solution)/shard_map/store/pallas_call | solution.py:756
